TPU v7x, 256 devices: a whole 4x4x8 slice. The times are simulated.
256 devices in a mesh: fsdp: 2 (over y_hi), dp: 32 (over x, z), owner: 4 (over y_lo, core).
Axes of the slice: x: 4, y: 4 (y_hi: 2, y_lo: 2; y = y_hi * 2 + y_lo), z: 8, core: 2. Of those that a mesh axis runs over, the one named last changes fastest.
Arguments:
- hidden: bfloat16 [256, 256, 4096], P(('fsdp', 'dp', 'owner')), may hold values from -6 to 6
- norm_gain: float32 [4096], replicated, may hold values from 0.1 to 1.9
- query_weight: bfloat16 [4096, 2048], P(('fsdp', 'dp')), may hold values from -0.09375 to 0.09375
- key_value_weight: bfloat16 [4096, 1024], P(('fsdp', 'dp')), may hold values from -0.09375 to 0.09375
- lengths: int32 [256], P(('fsdp', 'dp', 'owner')), may hold values from 128 to 256, as said below
- cotangent: bfloat16 [256, 256, 2048], P(('fsdp', 'dp', 'owner')), may hold values from -6 to 6
- cartridge: float32 [512, 1024], P('owner'), may hold values from -48 to 48
- adam_first_moment: float32 [512, 1024], P('owner'), may hold values from -6 to 6
- adam_second_moment: float32 [512, 1024], P('owner'), may hold values from 0.01 to 1
Outputs:
- attention_out: bfloat16 [256, 256, 2048], P(('fsdp', 'dp', 'owner'))
- new_cartridge: float32 [512, 1024], P('owner')
- new_first: float32 [512, 1024], P('owner')
- new_second: float32 [512, 1024], P('owner')
Inputs may be any that keep to these rules, and one draw needn't show every extreme that they name: `lengths`: each conversation's live tokens are its first rows; the rows after them are padding; some conversation is full.
All inputs are finite; a program needn't handle non-finite values.
Results may differ from a plain program's by a relative error of at most 0.008.
The roundings to bfloat16 on the way count: a program that leaves them out, or rounds other values in their place, can miss the bound.
Values may be sent and summed in bfloat16 or wider, within the bound.
No kernel may reach another device: no remote copies, remote signals or barrier semaphores. Data moves between devices by JAX's collectives and lax.ppermute only.
A program may use at most 128 MiB of HBM per device.

v0:
```python
import jax
import jax.numpy as jnp
from jax import lax
from jax.experimental import pallas as pl
from jax.experimental.pallas import tpu as pltpu
from jax.sharding import PartitionSpec as P


HEAD_SIZE = 128
GROUP = 4
STEP = 50
ROWS = 256
WIDTH = 4096
PREFIX = 512
COLS = 768
HALF = 384
MESH_AXES = ("fsdp", "dp", "owner")
X_SIZE, Z_SIZE = 4, 8
LOG2E = 1.4426950408889634


def coords(i):
    return i // 128, (i % 128) // 32, (i // 4) % 8, (i // 2) % 2, i % 2


def device_at(y_hi, x, z, y_lo, core):
    return y_hi * 128 + (x * 8 + z) * 4 + y_lo * 2 + core


def permute(value, move):
    pairs = [(i, device_at(*move(*coords(i)))) for i in range(256)]
    return lax.ppermute(value, MESH_AXES, pairs)


def along_z(step):
    return lambda y_hi, x, z, y_lo, core: (y_hi, x, (z + step) % Z_SIZE, y_lo, core)


def along_x(step):
    return lambda y_hi, x, z, y_lo, core: (y_hi, (x + step) % X_SIZE, z, y_lo, core)


def other_core(y_hi, x, z, y_lo, core):
    return y_hi, x, z, y_lo, 1 - core


def pair_chip(y_hi, x, z, y_lo, core):
    return y_hi, x, z, 1 - y_lo, core


def across_y(y_hi, x, z, y_lo, core):
    return 1 - y_hi, x, z, 1 - y_lo, core


def spread(value, axes, members):
    copies = jnp.broadcast_to(value[None], (members,) + value.shape)
    return lax.all_to_all(copies, axes, 0, 0, tiled=True)


def rope_tables():
    exponent = jnp.arange(HEAD_SIZE // 2, dtype=jnp.float32) * (2.0 / HEAD_SIZE)
    inverse = jnp.power(jnp.float32(500000.0), -exponent)
    position = (PREFIX + jnp.arange(ROWS)).astype(jnp.float32)
    angles = position[:, None] * inverse[None, :]
    cosine, sine = jnp.cos(angles), jnp.sin(angles)
    return (
        jnp.concatenate([cosine, cosine], axis=1),
        jnp.concatenate([-sine, sine], axis=1),
    )


def dot(a, b, a_dim, b_dim):
    return lax.dot_general(
        a, b, (((a_dim,), (b_dim,)), ((), ())), preferred_element_type=jnp.float32
    )


def norm_kernel(states, gain, normed):
    wide = states[0].astype(jnp.float32)
    scale = lax.rsqrt(jnp.mean(wide * wide, axis=1, keepdims=True) + 1e-05)
    normed[...] = (wide * scale * gain[...]).astype(jnp.bfloat16)


def normalise(hidden, gain, half):
    return pl.pallas_call(
        norm_kernel,
        grid=(2,),
        in_specs=[
            pl.BlockSpec((1, 64, WIDTH), lambda i: (0, 2 * half + i, 0)),
            pl.BlockSpec((1, WIDTH), lambda i: (0, 0)),
        ],
        out_specs=pl.BlockSpec((64, WIDTH), lambda i: (i, 0)),
        out_shape=jax.ShapeDtypeStruct((ROWS // 2, WIDTH), jnp.bfloat16),
    )(hidden, gain.reshape(1, WIDTH))


def live(length):
    return lax.broadcasted_iota(jnp.int32, (ROWS, 512), 0) < length


def pack_kernel(place, cotangent, key_rows, value_rows, *packed):
    for index in range(4):

        @pl.when(pl.program_id(0) == index)
        def _():
            target = packed[index] if index < 2 else packed[2].at[index - 2]
            target[0:ROWS, :] = jnp.where(live(place[4]), cotangent[0], 0).astype(jnp.bfloat16)
            for half in range(2):
                rows = slice(half * 64, half * 64 + 64)
                target[ROWS:, half * 128 : half * 128 + 128] = key_rows[rows, :].astype(
                    jnp.bfloat16
                )
                target[ROWS:, 256 + half * 128 : 384 + half * 128] = value_rows[rows, :].astype(
                    jnp.bfloat16
                )


def pack(place, cotangent, cartridge):
    return pl.pallas_call(
        pack_kernel,
        grid_spec=pltpu.PrefetchScalarGridSpec(
            num_scalar_prefetch=1,
            grid=(4,),
            in_specs=[
                pl.BlockSpec((1, ROWS, 512), lambda i, place: (0, 0, place[0] ^ i)),
                pl.BlockSpec((128, 128), lambda i, place: (0, place[0] ^ i)),
                pl.BlockSpec((128, 128), lambda i, place: (0, 4 + (place[0] ^ i))),
            ],
            out_specs=[pl.BlockSpec((320, 512), lambda i, place: (0, 0))] * 2
            + [pl.BlockSpec((2, 320, 512), lambda i, place: (0, 0, 0))],
        ),
        out_shape=[jax.ShapeDtypeStruct((320, 512), jnp.bfloat16)] * 2
        + [jax.ShapeDtypeStruct((2, 320, 512), jnp.bfloat16)],
    )(place, cotangent, cartridge, cartridge)


def unpack_kernel(place, *refs):
    out = refs[4]
    for index in range(4):

        @pl.when(pl.program_id(0) == index)
        def _():
            out[0] = jnp.where(live(place[4]), refs[index][...], 0).astype(jnp.bfloat16)


def unpack(place, pieces):
    return pl.pallas_call(
        unpack_kernel,
        grid_spec=pltpu.PrefetchScalarGridSpec(
            num_scalar_prefetch=1,
            grid=(4,),
            in_specs=[pl.BlockSpec((ROWS, 512), lambda i, place: (0, 0))] * 2
            + [
                pl.BlockSpec((None, ROWS, 512), lambda i, place: (0, 0, 0)),
                pl.BlockSpec((None, ROWS, 512), lambda i, place: (1, 0, 0)),
            ],
            out_specs=pl.BlockSpec((1, ROWS, 512), lambda i, place: (0, 0, place[0] ^ i)),
        ),
        out_shape=jax.ShapeDtypeStruct((1, ROWS, 2048), jnp.bfloat16),
    )(place, *pieces)


def layer_kernel(place, *refs):
    states = refs[0:8]
    z_pieces = refs[8:16]
    x_pieces = refs[16:24]
    packed, cosine, sine = refs[24:28], refs[28], refs[29]
    outs, gradient = refs[30:33], refs[33]
    weights, rows, keys, values, ups, out, sums, piece_sem, row_sem, up_sem = refs[34:]
    step = pl.program_id(0)
    y_hi, x, z = place[1], place[2], place[3]

    def piece_copies():
        copies = []

        def add(source, target):
            copies.append(
                pltpu.make_async_copy(source, target, piece_sem.at[len(copies)])
            )

        offsets = (0, -1, 1, -2, 2, -3, 3, 4)
        for piece, offset in zip(z_pieces, offsets):
            z_from = lax.rem(z + (offset + Z_SIZE), Z_SIZE)
            for back in range(X_SIZE):
                x_from = lax.rem(x + (X_SIZE - back), X_SIZE)
                add(piece.at[back], weights.at[:, x_from, z_from, :, pl.ds(0, HALF)])
        for index, offset in enumerate((0, -1, 1, 2)):
            x_from = lax.rem(x + (offset + X_SIZE), X_SIZE)
            for order in range(Z_SIZE):
                z_from = lax.rem(z + (offsets[order] + Z_SIZE), Z_SIZE)
                piece = x_pieces[2 * index + (order >= 3)]
                add(
                    piece.at[order - 3 if order >= 3 else order],
                    weights.at[:, x_from, z_from, :, pl.ds(HALF, HALF)],
                )
        return copies

    def row_copies(index):
        slot = index % 2
        return [
            pltpu.make_async_copy(
                states[2 * index + half],
                rows.at[slot, pl.ds(half * 128, 128)],
                row_sem.at[slot, half],
            )
            for half in range(2)
        ]

    def up_copies():
        return [
            pltpu.make_async_copy(source, ups.at[index], up_sem.at[index])
            for index, source in enumerate(
                (packed[0], packed[1], packed[2].at[0], packed[3].at[1])
            )
        ]

    @pl.when(step == 0)
    def _():
        for copy in piece_copies():
            copy.start()
        for copy in row_copies(0) + row_copies(1):
            copy.start()
        for copy in up_copies():
            copy.start()
        sums[...] = jnp.zeros_like(sums)
        for copy in up_copies():
            copy.wait()
        for index in range(4):
            first = pl.multiple_of((place[0] ^ index) * 128, 128)
            for half in range(2):
                target = pl.ds(first + half * 64, 64)
                keys[target, :] = ups[index, ROWS:, half * 128 : half * 128 + 128]
                values[target, :] = ups[index, ROWS:, 256 + half * 128 : 384 + half * 128]
        for copy in piece_copies():
            copy.wait()

    for index in range(4):

        @pl.when(step == index)
        def _():
            if index in (1, 2):
                for copy in row_copies(index + 1):
                    copy.start()
            for copy in row_copies(index):
                copy.wait()

    slot = lax.rem(step, 2)
    projected = sum(
        dot(
            rows[slot, :, pl.ds(pl.multiple_of((y_hi ^ side) * 2048, 2048), 2048)],
            weights[side].reshape(2048, COLS),
            1,
            0,
        )
        for side in range(2)
    )
    cos, sin = cosine[...], sine[...]

    def rope(v):
        return (v * cos + pltpu.roll(v, HEAD_SIZE // 2, 1) * sin).astype(jnp.bfloat16)

    own_keys = rope(projected[:, 512:640])
    own_values = projected[:, 640:768].astype(jnp.bfloat16)
    prefix_keys, prefix_values = keys[...], values[...]
    causal = lax.broadcasted_iota(jnp.int32, (ROWS, ROWS), 0) >= lax.broadcasted_iota(
        jnp.int32, (ROWS, ROWS), 1
    )
    scale = HEAD_SIZE ** (-0.5) * LOG2E
    lanes = [slice(h * HEAD_SIZE, (h + 1) * HEAD_SIZE) for h in range(GROUP)]
    queries = [rope(projected[:, lane]) for lane in lanes]
    key_sum = jnp.zeros((HEAD_SIZE, PREFIX), jnp.float32)
    value_sum = jnp.zeros((HEAD_SIZE, PREFIX), jnp.float32)

    def scores(head):
        return dot(queries[head], prefix_keys, 1, 1), dot(queries[head], own_keys, 1, 1)

    def soft(ready):
        before, own = ready
        own = jnp.where(causal, own, -1e30)
        highest = jnp.maximum(
            jnp.max(before, axis=1, keepdims=True), jnp.max(own, axis=1, keepdims=True)
        )
        before = jnp.exp2((before - highest) * scale)
        own = jnp.exp2((own - highest) * scale)
        total = jnp.sum(before, axis=1, keepdims=True) + jnp.sum(own, axis=1, keepdims=True)
        inverse = 1.0 / total
        probs = before * inverse
        return probs, probs.astype(jnp.bfloat16), (own * inverse).astype(jnp.bfloat16)

    def attend(head, soft_out):
        _, probs_low, own_low = soft_out
        upstream = ups[step, 0:ROWS, lanes[head]]
        attended = (
            dot(probs_low, prefix_values, 1, 0) + dot(own_low, own_values, 1, 0)
        ).astype(jnp.bfloat16)
        out[:, lanes[head]] = attended
        return attended, dot(upstream, prefix_values, 1, 1), dot(upstream, probs_low, 0, 0)

    def back(head, probs, attended, dprob):
        upstream = ups[step, 0:ROWS, lanes[head]]
        delta = jnp.sum(
            upstream.astype(jnp.float32) * attended.astype(jnp.float32),
            axis=1,
            keepdims=True,
        )
        dscore = (probs * (dprob - delta)).astype(jnp.bfloat16)
        return dot(queries[head], dscore, 0, 0)

    score_out, soft_out, attend_out = {}, {}, {}
    for tick in range(GROUP + 3):
        if tick < GROUP:
            score_out[tick] = scores(tick)
        if 0 <= tick - 2 < GROUP:
            attend_out[tick - 2] = attend(tick - 2, soft_out[tick - 2])
            value_sum += attend_out[tick - 2][2]
        if 0 <= tick - 1 < GROUP:
            soft_out[tick - 1] = soft(score_out[tick - 1])
        if 0 <= tick - 3 < GROUP:
            attended, dprob, _ = attend_out[tick - 3]
            key_sum += back(tick - 3, soft_out[tick - 3][0], attended, dprob)
    sums[0:HEAD_SIZE, :] += key_sum * HEAD_SIZE ** (-0.5)
    sums[HEAD_SIZE:, :] += value_sum

    for index in range(4):

        @pl.when(step == index)
        def _():
            target = outs[index] if index < 2 else outs[2].at[index - 2]
            target[...] = out[...]

    @pl.when(step == 3)
    def _():
        gradient[...] = sums[...].T.astype(gradient.dtype)


def layer(place, states, z_pieces, x_pieces, packed, cosine, sine):
    anywhere = pl.BlockSpec(memory_space=pl.ANY)

    def whole(shape):
        return pl.BlockSpec(
            shape, lambda i, place: (0,) * len(shape), pipeline_mode=pl.Buffered(1)
        )

    return pl.pallas_call(
        layer_kernel,
        grid_spec=pltpu.PrefetchScalarGridSpec(
            num_scalar_prefetch=1,
            grid=(4,),
            in_specs=[anywhere] * 28 + [whole(cosine.shape), whole(sine.shape)],
            out_specs=[pl.BlockSpec((ROWS, 512), lambda i, place: (0, 0))] * 2
            + [
                pl.BlockSpec((2, ROWS, 512), lambda i, place: (0, 0, 0)),
                pl.BlockSpec((PREFIX, 256), lambda i, place: (0, 0)),
            ],
            scratch_shapes=[
                pltpu.VMEM((2, X_SIZE, Z_SIZE, 64, COLS), jnp.bfloat16),
                pltpu.VMEM((2, ROWS, WIDTH), jnp.bfloat16),
                pltpu.VMEM((PREFIX, HEAD_SIZE), jnp.bfloat16),
                pltpu.VMEM((PREFIX, HEAD_SIZE), jnp.bfloat16),
                pltpu.VMEM((4, 320, 512), jnp.bfloat16),
                pltpu.VMEM((ROWS, 512), jnp.bfloat16),
                pltpu.VMEM((256, PREFIX), jnp.float32),
                pltpu.SemaphoreType.DMA((64,)),
                pltpu.SemaphoreType.DMA((2, 2)),
                pltpu.SemaphoreType.DMA((4,)),
            ],
        ),
        out_shape=[jax.ShapeDtypeStruct((ROWS, 512), jnp.bfloat16)] * 2
        + [
            jax.ShapeDtypeStruct((2, ROWS, 512), jnp.bfloat16),
            jax.ShapeDtypeStruct((PREFIX, 256), jnp.bfloat16),
        ],
        compiler_params=pltpu.CompilerParams(dimension_semantics=("arbitrary",)),
    )(place, *states, *z_pieces, *x_pieces, *packed, cosine, sine)


def of_head(query_weight, key_value_weight, index):
    return jnp.concatenate(
        [
            lax.dynamic_slice_in_dim(query_weight, index * 512, 512, 1),
            lax.dynamic_slice_in_dim(key_value_weight, index * 128, 128, 1),
            lax.dynamic_slice_in_dim(key_value_weight, 512 + index * 128, 128, 1),
        ],
        axis=1,
    )


def gather_weights(own, across):
    both = jnp.stack([own, across])
    first, second = both[:, :, :HALF], both[:, :, HALF:]
    ups, downs = [second], [second]
    for _ in range(3):
        ups.append(permute(ups[-1], along_z(1)))
        downs.append(permute(downs[-1], along_z(-1)))
    last = permute(ups[3], along_z(1))
    near = jnp.stack([second, ups[1], downs[1]])
    rest = jnp.stack([ups[2], downs[2], ups[3], downs[3], last])
    near_up, near_down = permute(near, along_x(1)), permute(near, along_x(-1))
    rest_up, rest_down = permute(rest, along_x(1)), permute(rest, along_x(-1))
    near_two = permute(near_up, along_x(1))
    rest_two = permute(rest_down, along_x(-1))
    x_pieces = [near, rest, near_up, rest_up, near_down, rest_down, near_two, rest_two]
    block = jnp.stack([first] + [permute(first, along_x(step)) for step in (1, 2, 3)])
    z_pieces = [block]
    up, down = block, block
    for _ in range(3):
        up, down = permute(up, along_z(1)), permute(down, along_z(-1))
        z_pieces += [up, down]
    z_pieces += [permute(up, along_z(1))]
    return z_pieces, x_pieces


def adam_update(current, moment_one, moment_two, prefix_gradient):
    one_new = 0.9 * moment_one + 0.1 * prefix_gradient
    two_new = 0.999 * moment_two + 0.001 * prefix_gradient * prefix_gradient
    one_fix = 1.0 - 0.9**STEP
    two_fix = 1.0 - 0.999**STEP
    updated = current - 0.02 * (one_new / one_fix) / (jnp.sqrt(two_new / two_fix) + 1e-08)
    return (updated, one_new, two_new)


def layer_step(
    hidden,
    norm_gain,
    query_weight,
    key_value_weight,
    lengths,
    cotangent,
    cartridge,
    adam_first_moment,
    adam_second_moment,
):
    head = lax.axis_index("owner")
    replica = lax.axis_index("dp")
    cosine, sine = rope_tables()
    place = jnp.stack(
        [head, lax.axis_index("fsdp"), replica // Z_SIZE, replica % Z_SIZE, lengths[0]]
    ).astype(jnp.int32)
    sent = of_head(query_weight, key_value_weight, head ^ 2)
    own = of_head(query_weight, key_value_weight, head)
    own, sent, hidden = lax.optimization_barrier((own, sent, hidden))
    across = permute(sent, across_y)
    states = {}
    for half in range(2):
        normed = normalise(hidden, norm_gain, half)
        far = permute(normed, pair_chip)
        states[half] = (normed, permute(normed, other_core), far, permute(far, other_core))
    z_pieces, x_pieces = gather_weights(own, across)
    own_part, near_part, pair_part = pack(place, cotangent, cartridge)
    pair_part = permute(pair_part, pair_chip)
    packed = (own_part, permute(near_part, other_core), pair_part, permute(pair_part, other_core))
    states = [states[half][index] for index in range(4) for half in range(2)]
    own_out, near_out, pair_out, gradient = layer(
        place, states, z_pieces, x_pieces, packed, cosine, sine
    )
    pair_out = permute(pair_out, pair_chip)
    returned = (own_out, permute(near_out, other_core), pair_out, permute(pair_out, other_core))
    terms = lax.all_to_all(gradient.reshape(256, 2, 256), ("owner", "fsdp", "dp"), 0, 0, tiled=True)
    summed = jnp.sum(terms.reshape(4, 64, 2, 2, 128).astype(jnp.float32), axis=1)
    summed = summed.transpose(1, 2, 0, 3).reshape(2, 1024)
    owned = spread(summed.astype(jnp.bfloat16), ("fsdp", "dp"), 64)
    owned = owned.reshape(128, 1024).astype(jnp.float32)
    attention_out = unpack(place, returned)
    new_cartridge, new_first, new_second = adam_update(
        cartridge, adam_first_moment, adam_second_moment, owned
    )
    return attention_out, new_cartridge, new_first, new_second


def solution(mesh):
    placed = (
        P(MESH_AXES, None, None),
        P(),
        P(("fsdp", "dp"), None),
        P(("fsdp", "dp"), None),
        P(MESH_AXES),
        P(MESH_AXES, None, None),
        P("owner", None),
        P("owner", None),
        P("owner", None),
    )
    return jax.shard_map(
        layer_step,
        mesh=mesh,
        in_specs=placed,
        out_specs=(
            P(MESH_AXES, None, None),
            P("owner", None),
            P("owner", None),
            P("owner", None),
        ),
        check_vma=False,
    )
```

profile of v0, /device:TPU:2, one launch (start us, length us, event | category | flops | bytes accessed | tf_op | source)
XLA Modules:
  0.0 219.3 jit_solution(8581149347141620871)
XLA Ops:
  2.4 3.1 %collective-permute-start.6 = (bf16[64,768]{1,0:T(8,128)(2,1)S(1)}, bf16[64,768]{1,0:T(8,128)(2,1)S(1)}, u32[]{:S(2)}, u32[]{:S(2)}) collective-permute-start(bf16[64,768]{1,0:T(8,128)(2,1)S(1)} %get-tuple-element.16), channel_id=1, source_target_pairs={{0,130},{1,131},{2,128},{3,129},{4,134},{5,135},{6,132},{7,133},{8... | collective-permute-start | bytes 294920 | tf_op jit(solution)/shard_map/ppermute | solution.py:32
  5.5 2.8 %collective-permute-done.6 = bf16[64,768]{1,0:T(8,128)(2,1)S(1)} collective-permute-done((bf16[64,768]{1,0:T(8,128)(2,1)S(1)}, bf16[64,768]{1,0:T(8,128)(2,1)S(1)}, u32[]{:S(2)}, u32[]{:S(2)}) %collective-permute-start.6) | collective-permute-done | bytes 98336 | tf_op jit(solution)/shard_map/ppermute | solution.py:32
  8.3 2.0 collective-permute-start.17
  10.3 4.0 %collective-permute-start.18 = (bf16[2,64,384]{2,1,0:T(8,128)(2,1)S(1)}, bf16[2,64,384]{2,1,0:T(8,128)(2,1)S(1)}, u32[]{:S(2)}, u32[]{:S(2)}) collective-permute-start(bf16[2,64,384]{2,1,0:T(8,128)(2,1)S(1)} %get-tuple-element.29), channel_id=1, source_target_pairs={{0,28},{1,29},{2,30},{3,31},{4,0},{5,1},{6,2},{7,3},{8,4},{9,5},{1... | collective-permute-start | bytes 294920 | tf_op jit(solution)/shard_map/ppermute | solution.py:32
  15.6 4.0 %shard_map.122 = (bf16[320,512]{1,0:T(8,128)(2,1)}, bf16[320,512]{1,0:T(8,128)(2,1)}, bf16[2,320,512]{2,1,0:T(8,128)(2,1)}) custom-call(s32[5]{0:T(128)} %stack.73.place, bf16[1,256,2048]{2,1,0:T(8,128)(2,1)} %cotangent.1, f32[128,1024]{1,0:T(8,128)} %value_rows.1, f32[128,1024]{1,0:T(8,128)} %value_rows.1), custom_call_target="tpu_custom_call" | custom-call | tf_op jit(solution)/shard_map/pallas_call | solution.py:119
  20.5 2.4 %collective-permute-start.8 = (bf16[2,64,384]{2,1,0:T(8,128)(2,1)S(1)}, bf16[2,64,384]{2,1,0:T(8,128)(2,1)S(1)}, u32[]{:S(2)}, u32[]{:S(2)}) collective-permute-start(bf16[2,64,384]{2,1,0:T(8,128)(2,1)S(1)} %get-tuple-element.30), channel_id=1, source_target_pairs={{0,64},{1,65},{2,66},{3,67},{4,68},{5,69},{6,70},{7,71},{8,72},{9,... | collective-permute-start | bytes 294920 | tf_op jit(solution)/shard_map/ppermute | solution.py:32
  24.9 2.2 %collective-permute-start.24 = (bf16[3,2,64,384]{3,2,1,0:T(8,128)(2,1)S(1)}, bf16[3,2,64,384]{3,2,1,0:T(8,128)(2,1)}, u32[]{:S(2)}, u32[]{:S(2)}) collective-permute-start(bf16[3,2,64,384]{3,2,1,0:T(8,128)(2,1)S(1)} %pad_maximum_fusion.1.refs_16_), channel_id=1, source_target_pairs={{0,32},{1,33},{2,34},{3,35},{4,36},{5,37},{6,38},{7,39},{8,40},{9,... | collective-permute-start | bytes 884744 | tf_op jit(solution)/shard_map/ppermute | solution.py:32
  29.8 2.0 collective-permute-start.11
  31.8 2.0 collective-permute-done.19
  35.1 6.1 %collective-permute-done.20 = bf16[2,64,384]{2,1,0:T(8,128)(2,1)S(1)} collective-permute-done((bf16[2,64,384]{2,1,0:T(8,128)(2,1)S(1)}, bf16[2,64,384]{2,1,0:T(8,128)(2,1)S(1)}, u32[]{:S(2)}, u32[]{:S(2)}) %collective-permute-start.20) | collective-permute-done | bytes 98336 | tf_op jit(solution)/shard_map/ppermute | solution.py:32
  42.2 3.2 %collective-permute-start.22 = (bf16[2,64,384]{2,1,0:T(8,128)(2,1)S(1)}, bf16[2,64,384]{2,1,0:T(8,128)(2,1)S(1)}, u32[]{:S(2)}, u32[]{:S(2)}) collective-permute-start(bf16[2,64,384]{2,1,0:T(8,128)(2,1)S(1)} %collective-permute-done.20), channel_id=1, source_target_pairs={{0,28},{1,29},{2,30},{3,31},{4,0},{5,1},{6,2},{7,3},{8,4},{9,5},{1... | collective-permute-start | bytes 294920 | tf_op jit(solution)/shard_map/ppermute | solution.py:32
  45.4 1.9 collective-permute-done.21
  48.0 3.2 %collective-permute-start.26 = (bf16[3,2,64,384]{3,2,1,0:T(8,128)(2,1)S(1)}, bf16[3,2,64,384]{3,2,1,0:T(8,128)(2,1)S(1)}, u32[]{:S(2)}, u32[]{:S(2)}) collective-permute-start(bf16[3,2,64,384]{3,2,1,0:T(8,128)(2,1)S(1)} %pad_maximum_fusion.1.refs_16_), channel_id=1, source_target_pairs={{0,96},{1,97},{2,98},{3,99},{4,100},{5,101},{6,102},{7,103},{8,104... | collective-permute-start | bytes 884744 | tf_op jit(solution)/shard_map/ppermute | solution.py:32
  51.2 2.4 %collective-permute-done.23 = bf16[2,64,384]{2,1,0:T(8,128)(2,1)S(1)} collective-permute-done((bf16[2,64,384]{2,1,0:T(8,128)(2,1)S(1)}, bf16[2,64,384]{2,1,0:T(8,128)(2,1)S(1)}, u32[]{:S(2)}, u32[]{:S(2)}) %collective-permute-start.23) | collective-permute-done | bytes 98336 | tf_op jit(solution)/shard_map/ppermute | solution.py:32
  54.3 2.7 %collective-permute-start.28 = (bf16[3,2,64,384]{3,2,1,0:T(8,128)(2,1)}, bf16[3,2,64,384]{3,2,1,0:T(8,128)(2,1)}, u32[]{:S(2)}, u32[]{:S(2)}) collective-permute-start(bf16[3,2,64,384]{3,2,1,0:T(8,128)(2,1)} %collective-permute-done.24.refs_18_), channel_id=1, source_target_pairs={{0,32},{1,33},{2,34},{3,35},{4,36},{5,37},{6,38},{7,39},{8,40},{9,... | collective-permute-start | bytes 884744 | tf_op jit(solution)/shard_map/ppermute | solution.py:32
  57.0 3.1 %collective-permute-start.13 = (bf16[4,2,64,384]{3,2,1,0:T(8,128)(2,1)S(1)}, bf16[4,2,64,384]{3,2,1,0:T(8,128)(2,1)}, u32[]{:S(2)}, u32[]{:S(2)}) collective-permute-start(bf16[4,2,64,384]{3,2,1,0:T(8,128)(2,1)S(1)} %collective-permute-done.11.refs_10_), channel_id=1, source_target_pairs={{0,28},{1,29},{2,30},{3,31},{4,0},{5,1},{6,2},{7,3},{8,4},{9,5},{1... | collective-permute-start | bytes 1179656 | tf_op jit(solution)/shard_map/ppermute | solution.py:32
  61.4 2.4 %shard_map.121.refs_1_ = bf16[128,4096]{1,0:T(8,128)(2,1)} custom-call(bf16[1,256,4096]{2,1,0:T(8,128)(2,1)} %states.1, f32[1,4096]{1,0:T(1,128)} %bitcast.34), custom_call_target="tpu_custom_call" | custom-call | tf_op jit(solution)/shard_map/pallas_call | solution.py:85
  63.8 2.5 %shard_map.120.refs_0_ = bf16[128,4096]{1,0:T(8,128)(2,1)} custom-call(bf16[1,256,4096]{2,1,0:T(8,128)(2,1)} %states.1, f32[1,4096]{1,0:T(1,128)} %bitcast.35), custom_call_target="tpu_custom_call" | custom-call | tf_op jit(solution)/shard_map/pallas_call | solution.py:85
  68.6 9.1 %collective-permute-done.12.refs_11_ = bf16[4,2,64,384]{3,2,1,0:T(8,128)(2,1)S(1)} collective-permute-done((bf16[4,2,64,384]{3,2,1,0:T(8,128)(2,1)}, bf16[4,2,64,384]{3,2,1,0:T(8,128)(2,1)S(1)}, u32[]{:S(2)}, u32[]{:S(2)}) %collective-permute-start.12) | collective-permute-done | bytes 393248 | tf_op jit(solution)/shard_map/ppermute | solution.py:32
  79.1 13.5 %collective-permute-done.25.refs_19_ = bf16[5,2,64,384]{3,2,1,0:T(8,128)(2,1)S(1)} collective-permute-done((bf16[5,2,64,384]{3,2,1,0:T(8,128)(2,1)}, bf16[5,2,64,384]{3,2,1,0:T(8,128)(2,1)S(1)}, u32[]{:S(2)}, u32[]{:S(2)}) %collective-permute-start.25) | collective-permute-done | bytes 491552 | tf_op jit(solution)/shard_map/ppermute | solution.py:32
  93.1 16.6 %collective-permute-done.3.refs_5_ = bf16[128,4096]{1,0:T(8,128)(2,1)S(1)} collective-permute-done((bf16[128,4096]{1,0:T(8,128)(2,1)S(1)}, bf16[128,4096]{1,0:T(8,128)(2,1)S(1)}, u32[]{:S(2)}, u32[]{:S(2)}) %collective-permute-start.3) | collective-permute-done | bytes 1048608 | tf_op jit(solution)/shard_map/ppermute | solution.py:32
  111.7 2.9 %collective-permute-start.29 = (bf16[5,2,64,384]{3,2,1,0:T(8,128)(2,1)}, bf16[5,2,64,384]{3,2,1,0:T(8,128)(2,1)S(1)}, u32[]{:S(2)}, u32[]{:S(2)}) collective-permute-start(bf16[5,2,64,384]{3,2,1,0:T(8,128)(2,1)} %collective-permute-done.27.refs_21_), channel_id=1, source_target_pairs={{0,96},{1,97},{2,98},{3,99},{4,100},{5,101},{6,102},{7,103},{8,104... | collective-permute-start | bytes 1474568 | tf_op jit(solution)/shard_map/ppermute | solution.py:32
  114.6 2.4 %collective-permute-start.15 = (bf16[4,2,64,384]{3,2,1,0:T(8,128)(2,1)}, bf16[4,2,64,384]{3,2,1,0:T(8,128)(2,1)S(1)}, u32[]{:S(2)}, u32[]{:S(2)}) collective-permute-start(bf16[4,2,64,384]{3,2,1,0:T(8,128)(2,1)} %collective-permute-done.13.refs_12_), channel_id=1, source_target_pairs={{0,28},{1,29},{2,30},{3,31},{4,0},{5,1},{6,2},{7,3},{8,4},{9,5},{1... | collective-permute-start | bytes 1179656 | tf_op jit(solution)/shard_map/ppermute | solution.py:32
  117.0 5.5 %collective-permute-done.14.refs_13_ = bf16[4,2,64,384]{3,2,1,0:T(8,128)(2,1)S(1)} collective-permute-done((bf16[4,2,64,384]{3,2,1,0:T(8,128)(2,1)S(1)}, bf16[4,2,64,384]{3,2,1,0:T(8,128)(2,1)S(1)}, u32[]{:S(2)}, u32[]{:S(2)}) %collective-permute-start.14) | collective-permute-done | bytes 393248 | tf_op jit(solution)/shard_map/ppermute | solution.py:32
  123.9 2.2 %collective-permute-done.15.refs_14_ = bf16[4,2,64,384]{3,2,1,0:T(8,128)(2,1)S(1)} collective-permute-done((bf16[4,2,64,384]{3,2,1,0:T(8,128)(2,1)}, bf16[4,2,64,384]{3,2,1,0:T(8,128)(2,1)S(1)}, u32[]{:S(2)}, u32[]{:S(2)}) %collective-permute-start.15) | collective-permute-done | bytes 393248 | tf_op jit(solution)/shard_map/ppermute | solution.py:32
  126.1 8.1 %collective-permute-done.16.refs_15_ = bf16[4,2,64,384]{3,2,1,0:T(8,128)(2,1)S(1)} collective-permute-done((bf16[4,2,64,384]{3,2,1,0:T(8,128)(2,1)S(1)}, bf16[4,2,64,384]{3,2,1,0:T(8,128)(2,1)S(1)}, u32[]{:S(2)}, u32[]{:S(2)}) %collective-permute-start.16) | collective-permute-done | bytes 393248 | tf_op jit(solution)/shard_map/ppermute | solution.py:32
  136.3 26.9 %shard_map.123 = (bf16[256,512]{1,0:T(8,128)(2,1)}, bf16[256,512]{1,0:T(8,128)(2,1)}, bf16[2,256,512]{2,1,0:T(8,128)(2,1)}, bf16[512,256]{1,0:T(8,128)(2,1)}) custom-call(s32[5]{0:T(128)} %stack.73.place, bf16[128,4096]{1,0:T(8,128)(2,1)} %shard_map.120.refs_0_, bf16[128,4096]{1,0:T(8,128)(2,1)} %shard_map.121.refs_1_, bf16[128,4096]{1,0:T(8,128)(2,1)} %copy-done.6, ...), custom_call_target="tpu_custom_call" | custom-call | tf_op jit(solution)/shard_map/pallas_call | solution.py:344
  165.1 13.2 %all-to-all-start = ((bf16[256,2,256]{2,1,0:T(2,128)(2,1)}), bf16[256,2,256]{2,1,0:T(2,128)(2,1)S(1)}, u32[]{:S(2)}, u32[]{:S(2)}) async-start(bf16[256,2,256]{2,1,0:T(2,128)(2,1)} %reshape.40), calls=%async_computation | async-start | bytes 524288 | tf_op jit(solution)/shard_map/all_to_all | solution.py:458
  179.9 13.3 %all-to-all-done = bf16[256,2,256]{2,1,0:T(2,128)(2,1)S(1)} async-done(((bf16[256,2,256]{2,1,0:T(2,128)(2,1)}), bf16[256,2,256]{2,1,0:T(2,128)(2,1)S(1)}, u32[]{:S(2)}, u32[]{:S(2)}) %all-to-all-start) | async-done | bytes 262176 | tf_op jit(solution)/shard_map/all_to_all | solution.py:458
  194.4 5.9 %all-to-all-start.1 = ((bf16[64,2,1024]{2,1,0:T(2,128)(2,1)}), bf16[64,2,1024]{2,1,0:T(2,128)(2,1)S(1)}, u32[]{:S(2)}, u32[]{:S(2)}) async-start(bf16[64,2,1024]{2,1,0:T(2,128)(2,1)} %broadcast_in_dim.2), calls=%async_computation.1 | async-start | bytes 524288 | tf_op jit(solution)/shard_map/all_to_all | solution.py:57
  200.9 12.6 %all-to-all-done.1 = bf16[64,2,1024]{2,1,0:T(2,128)(2,1)S(1)} async-done(((bf16[64,2,1024]{2,1,0:T(2,128)(2,1)}), bf16[64,2,1024]{2,1,0:T(2,128)(2,1)S(1)}, u32[]{:S(2)}, u32[]{:S(2)}) %all-to-all-start.1) | async-done | bytes 262176 | tf_op jit(solution)/shard_map/all_to_all | solution.py:57
  215.8 3.5 %shard_map.124 = bf16[1,256,2048]{2,1,0:T(8,128)(2,1)} custom-call(s32[5]{0:T(128)} %stack.73.place, bf16[256,512]{1,0:T(8,128)(2,1)} %get-tuple-element.20.refs_0_, bf16[256,512]{1,0:T(8,128)(2,1)} %collective-permute-done.33.refs_1_, bf16[2,256,512]{2,1,0:T(8,128)(2,1)} %copy-done.13, bf16[2,256,512]{2,1,0:T(8,128)(2,1)} %copy-done.14), custom_call_target="tpu_custom_call" | custom-call | tf_op jit(solution)/shard_map/pallas_call | solution.py:147
  (121 shorter events, 29.9 us)
Async XLA Ops:
  8.3 12.2 %collective-permute-start.17 = (bf16[2,64,384]{2,1,0:T(8,128)(2,1)S(1)}, bf16[2,64,384]{2,1,0:T(8,128)(2,1)S(1)}, u32[]{:S(2)}, u32[]{:S(2)}) collective-permute-start(bf16[2,64,384]{2,1,0:T(8,128)(2,1)S(1)} %get-tuple-element.29), channel_id=1, source_target_pairs={{0,4},{1,5},{2,6},{3,7},{4,8},{5,9},{6,10},{7,11},{8,12},{9,13},{1... | collective-permute-start | bytes 294920 | tf_op jit(solution)/shard_map/ppermute | solution.py:32
  10.3 12.7 %collective-permute-start.18 = (bf16[2,64,384]{2,1,0:T(8,128)(2,1)S(1)}, bf16[2,64,384]{2,1,0:T(8,128)(2,1)S(1)}, u32[]{:S(2)}, u32[]{:S(2)}) collective-permute-start(bf16[2,64,384]{2,1,0:T(8,128)(2,1)S(1)} %get-tuple-element.29), channel_id=1, source_target_pairs={{0,28},{1,29},{2,30},{3,31},{4,0},{5,1},{6,2},{7,3},{8,4},{9,5},{1... | collective-permute-start | bytes 294920 | tf_op jit(solution)/shard_map/ppermute | solution.py:32
  19.6 22.6 %collective-permute-start.30 = (bf16[320,512]{1,0:T(8,128)(2,1)}, bf16[320,512]{1,0:T(8,128)(2,1)S(1)}, u32[]{:S(2)}, u32[]{:S(2)}) collective-permute-start(bf16[320,512]{1,0:T(8,128)(2,1)} %get-tuple-element.18), channel_id=1, source_target_pairs={{0,1},{1,0},{2,3},{3,2},{4,5},{5,4},{6,7},{7,6},{8,9},{9,8},{10,11... | collective-permute-start | bytes 983048 | tf_op jit(solution)/shard_map/ppermute | solution.py:32
  19.6 48.5 %collective-permute-start.31 = (bf16[2,320,512]{2,1,0:T(8,128)(2,1)}, bf16[2,320,512]{2,1,0:T(8,128)(2,1)}, u32[]{:S(2)}, u32[]{:S(2)}) collective-permute-start(bf16[2,320,512]{2,1,0:T(8,128)(2,1)} %get-tuple-element.19), channel_id=1, source_target_pairs={{0,2},{1,3},{2,0},{3,1},{4,6},{5,7},{6,4},{7,5},{8,10},{9,11},{10,... | collective-permute-start | bytes 1966088 | tf_op jit(solution)/shard_map/ppermute | solution.py:32
  20.5 7.4 %collective-permute-start.8 = (bf16[2,64,384]{2,1,0:T(8,128)(2,1)S(1)}, bf16[2,64,384]{2,1,0:T(8,128)(2,1)S(1)}, u32[]{:S(2)}, u32[]{:S(2)}) collective-permute-start(bf16[2,64,384]{2,1,0:T(8,128)(2,1)S(1)} %get-tuple-element.30), channel_id=1, source_target_pairs={{0,64},{1,65},{2,66},{3,67},{4,68},{5,69},{6,70},{7,71},{8,72},{9,... | collective-permute-start | bytes 294920 | tf_op jit(solution)/shard_map/ppermute | solution.py:32
  22.9 6.8 %collective-permute-start.7 = (bf16[2,64,384]{2,1,0:T(8,128)(2,1)S(1)}, bf16[2,64,384]{2,1,0:T(8,128)(2,1)S(1)}, u32[]{:S(2)}, u32[]{:S(2)}) collective-permute-start(bf16[2,64,384]{2,1,0:T(8,128)(2,1)S(1)} %get-tuple-element.30), channel_id=1, source_target_pairs={{0,32},{1,33},{2,34},{3,35},{4,36},{5,37},{6,38},{7,39},{8,40},{9,... | collective-permute-start | bytes 294920 | tf_op jit(solution)/shard_map/ppermute | solution.py:32
  24.9 29.4 %collective-permute-start.24 = (bf16[3,2,64,384]{3,2,1,0:T(8,128)(2,1)S(1)}, bf16[3,2,64,384]{3,2,1,0:T(8,128)(2,1)}, u32[]{:S(2)}, u32[]{:S(2)}) collective-permute-start(bf16[3,2,64,384]{3,2,1,0:T(8,128)(2,1)S(1)} %pad_maximum_fusion.1.refs_16_), channel_id=1, source_target_pairs={{0,32},{1,33},{2,34},{3,35},{4,36},{5,37},{6,38},{7,39},{8,40},{9,... | collective-permute-start | bytes 884744 | tf_op jit(solution)/shard_map/ppermute | solution.py:32
  29.8 27.2 %collective-permute-start.11 = (bf16[4,2,64,384]{3,2,1,0:T(8,128)(2,1)S(1)}, bf16[4,2,64,384]{3,2,1,0:T(8,128)(2,1)S(1)}, u32[]{:S(2)}, u32[]{:S(2)}) collective-permute-start(bf16[4,2,64,384]{3,2,1,0:T(8,128)(2,1)S(1)} %pad_maximum_fusion.refs_8_), channel_id=1, source_target_pairs={{0,28},{1,29},{2,30},{3,31},{4,0},{5,1},{6,2},{7,3},{8,4},{9,5},{1... | collective-permute-start | bytes 1179656 | tf_op jit(solution)/shard_map/ppermute | solution.py:32
  33.8 7.5 %collective-permute-start.20 = (bf16[2,64,384]{2,1,0:T(8,128)(2,1)S(1)}, bf16[2,64,384]{2,1,0:T(8,128)(2,1)S(1)}, u32[]{:S(2)}, u32[]{:S(2)}) collective-permute-start(bf16[2,64,384]{2,1,0:T(8,128)(2,1)S(1)} %collective-permute-done.18), channel_id=1, source_target_pairs={{0,28},{1,29},{2,30},{3,31},{4,0},{5,1},{6,2},{7,3},{8,4},{9,5},{1... | collective-permute-start | bytes 294920 | tf_op jit(solution)/shard_map/ppermute | solution.py:32
  48.0 12.7 %collective-permute-start.26 = (bf16[3,2,64,384]{3,2,1,0:T(8,128)(2,1)S(1)}, bf16[3,2,64,384]{3,2,1,0:T(8,128)(2,1)S(1)}, u32[]{:S(2)}, u32[]{:S(2)}) collective-permute-start(bf16[3,2,64,384]{3,2,1,0:T(8,128)(2,1)S(1)} %pad_maximum_fusion.1.refs_16_), channel_id=1, source_target_pairs={{0,96},{1,97},{2,98},{3,99},{4,100},{5,101},{6,102},{7,103},{8,104... | collective-permute-start | bytes 884744 | tf_op jit(solution)/shard_map/ppermute | solution.py:32
  53.6 12.7 %collective-permute-start.10 = (bf16[4,2,64,384]{3,2,1,0:T(8,128)(2,1)S(1)}, bf16[4,2,64,384]{3,2,1,0:T(8,128)(2,1)}, u32[]{:S(2)}, u32[]{:S(2)}) collective-permute-start(bf16[4,2,64,384]{3,2,1,0:T(8,128)(2,1)S(1)} %pad_maximum_fusion.refs_8_), channel_id=1, source_target_pairs={{0,4},{1,5},{2,6},{3,7},{4,8},{5,9},{6,10},{7,11},{8,12},{9,13},{1... | collective-permute-start | bytes 1179656 | tf_op jit(solution)/shard_map/ppermute | solution.py:32
  54.3 14.2 %collective-permute-start.28 = (bf16[3,2,64,384]{3,2,1,0:T(8,128)(2,1)}, bf16[3,2,64,384]{3,2,1,0:T(8,128)(2,1)}, u32[]{:S(2)}, u32[]{:S(2)}) collective-permute-start(bf16[3,2,64,384]{3,2,1,0:T(8,128)(2,1)} %collective-permute-done.24.refs_18_), channel_id=1, source_target_pairs={{0,32},{1,33},{2,34},{3,35},{4,36},{5,37},{6,38},{7,39},{8,40},{9,... | collective-permute-start | bytes 884744 | tf_op jit(solution)/shard_map/ppermute | solution.py:32
  57.0 11.5 %collective-permute-start.13 = (bf16[4,2,64,384]{3,2,1,0:T(8,128)(2,1)S(1)}, bf16[4,2,64,384]{3,2,1,0:T(8,128)(2,1)}, u32[]{:S(2)}, u32[]{:S(2)}) collective-permute-start(bf16[4,2,64,384]{3,2,1,0:T(8,128)(2,1)S(1)} %collective-permute-done.11.refs_10_), channel_id=1, source_target_pairs={{0,28},{1,29},{2,30},{3,31},{4,0},{5,1},{6,2},{7,3},{8,4},{9,5},{1... | collective-permute-start | bytes 1179656 | tf_op jit(solution)/shard_map/ppermute | solution.py:32
  60.7 17.0 %collective-permute-start.27 = (bf16[5,2,64,384]{3,2,1,0:T(8,128)(2,1)}, bf16[5,2,64,384]{3,2,1,0:T(8,128)(2,1)}, u32[]{:S(2)}, u32[]{:S(2)}) collective-permute-start(bf16[5,2,64,384]{3,2,1,0:T(8,128)(2,1)} %bitcast_dynamic-update-slice_fusion.refs_17_), channel_id=1, source_target_pairs={{0,96},{1,97},{2,98},{3,99},{4,100},{5,101},{6,102},{7,103},{8,104... | collective-permute-start | bytes 1474568 | tf_op jit(solution)/shard_map/ppermute | solution.py:32
  66.4 26.3 %collective-permute-start.2 = (bf16[128,4096]{1,0:T(8,128)(2,1)}, bf16[128,4096]{1,0:T(8,128)(2,1)S(1)}, u32[]{:S(2)}, u32[]{:S(2)}) collective-permute-start(bf16[128,4096]{1,0:T(8,128)(2,1)} %shard_map.120.refs_0_), channel_id=1, source_target_pairs={{0,2},{1,3},{2,0},{3,1},{4,6},{5,7},{6,4},{7,5},{8,10},{9,11},{10,... | collective-permute-start | bytes 3145736 | tf_op jit(solution)/shard_map/ppermute | solution.py:32
  68.1 41.6 %collective-permute-start.3 = (bf16[128,4096]{1,0:T(8,128)(2,1)S(1)}, bf16[128,4096]{1,0:T(8,128)(2,1)S(1)}, u32[]{:S(2)}, u32[]{:S(2)}) collective-permute-start(bf16[128,4096]{1,0:T(8,128)(2,1)S(1)} %copy-done.1), channel_id=1, source_target_pairs={{0,2},{1,3},{2,0},{3,1},{4,6},{5,7},{6,4},{7,5},{8,10},{9,11},{10,... | collective-permute-start | bytes 3145736 | tf_op jit(solution)/shard_map/ppermute | solution.py:32
  68.5 9.2 %collective-permute-start.12 = (bf16[4,2,64,384]{3,2,1,0:T(8,128)(2,1)}, bf16[4,2,64,384]{3,2,1,0:T(8,128)(2,1)S(1)}, u32[]{:S(2)}, u32[]{:S(2)}) collective-permute-start(bf16[4,2,64,384]{3,2,1,0:T(8,128)(2,1)} %collective-permute-done.10.refs_9_), channel_id=1, source_target_pairs={{0,4},{1,5},{2,6},{3,7},{4,8},{5,9},{6,10},{7,11},{8,12},{9,13},{1... | collective-permute-start | bytes 1179656 | tf_op jit(solution)/shard_map/ppermute | solution.py:32
  68.5 41.2 %collective-permute-start = (bf16[128,4096]{1,0:T(8,128)(2,1)}, bf16[128,4096]{1,0:T(8,128)(2,1)S(1)}, u32[]{:S(2)}, u32[]{:S(2)}) collective-permute-start(bf16[128,4096]{1,0:T(8,128)(2,1)} %shard_map.120.refs_0_), channel_id=1, source_target_pairs={{0,1},{1,0},{2,3},{3,2},{4,5},{5,4},{6,7},{7,6},{8,9},{9,8},{10,11... | collective-permute-start | bytes 3145736 | tf_op jit(solution)/shard_map/ppermute | solution.py:32
  77.7 32.1 %collective-permute-start.1 = (bf16[128,4096]{1,0:T(8,128)(2,1)S(1)}, bf16[128,4096]{1,0:T(8,128)(2,1)S(1)}, u32[]{:S(2)}, u32[]{:S(2)}) collective-permute-start(bf16[128,4096]{1,0:T(8,128)(2,1)S(1)} %copy-done.1), channel_id=1, source_target_pairs={{0,1},{1,0},{2,3},{3,2},{4,5},{5,4},{6,7},{7,6},{8,9},{9,8},{10,11... | collective-permute-start | bytes 3145736 | tf_op jit(solution)/shard_map/ppermute | solution.py:32
  77.7 14.9 %collective-permute-start.25 = (bf16[5,2,64,384]{3,2,1,0:T(8,128)(2,1)}, bf16[5,2,64,384]{3,2,1,0:T(8,128)(2,1)S(1)}, u32[]{:S(2)}, u32[]{:S(2)}) collective-permute-start(bf16[5,2,64,384]{3,2,1,0:T(8,128)(2,1)} %bitcast_dynamic-update-slice_fusion.refs_17_), channel_id=1, source_target_pairs={{0,32},{1,33},{2,34},{3,35},{4,36},{5,37},{6,38},{7,39},{8,40},{9,... | collective-permute-start | bytes 1474568 | tf_op jit(solution)/shard_map/ppermute | solution.py:32
  92.5 22.1 %collective-permute-start.32 = (bf16[2,320,512]{2,1,0:T(8,128)(2,1)}, bf16[2,320,512]{2,1,0:T(8,128)(2,1)S(1)}, u32[]{:S(2)}, u32[]{:S(2)}) collective-permute-start(bf16[2,320,512]{2,1,0:T(8,128)(2,1)} %collective-permute-done.31.refs_26_), channel_id=1, source_target_pairs={{0,1},{1,0},{2,3},{3,2},{4,5},{5,4},{6,7},{7,6},{8,9},{9,8},{10,11... | collective-permute-start | bytes 1966088 | tf_op jit(solution)/shard_map/ppermute | solution.py:32
  92.7 41.6 %collective-permute-start.4 = (bf16[128,4096]{1,0:T(8,128)(2,1)S(1)}, bf16[128,4096]{1,0:T(8,128)(2,1)S(1)}, u32[]{:S(2)}, u32[]{:S(2)}) collective-permute-start(bf16[128,4096]{1,0:T(8,128)(2,1)S(1)} %collective-permute-done.2.refs_4_), channel_id=1, source_target_pairs={{0,1},{1,0},{2,3},{3,2},{4,5},{5,4},{6,7},{7,6},{8,9},{9,8},{10,11... | collective-permute-start | bytes 3145736 | tf_op jit(solution)/shard_map/ppermute | solution.py:32
  109.7 24.6 %collective-permute-start.5 = (bf16[128,4096]{1,0:T(8,128)(2,1)S(1)}, bf16[128,4096]{1,0:T(8,128)(2,1)S(1)}, u32[]{:S(2)}, u32[]{:S(2)}) collective-permute-start(bf16[128,4096]{1,0:T(8,128)(2,1)S(1)} %collective-permute-done.3.refs_5_), channel_id=1, source_target_pairs={{0,1},{1,0},{2,3},{3,2},{4,5},{5,4},{6,7},{7,6},{8,9},{9,8},{10,11... | collective-permute-start | bytes 3145736 | tf_op jit(solution)/shard_map/ppermute | solution.py:32
  109.7 12.7 %collective-permute-start.14 = (bf16[4,2,64,384]{3,2,1,0:T(8,128)(2,1)S(1)}, bf16[4,2,64,384]{3,2,1,0:T(8,128)(2,1)S(1)}, u32[]{:S(2)}, u32[]{:S(2)}) collective-permute-start(bf16[4,2,64,384]{3,2,1,0:T(8,128)(2,1)S(1)} %collective-permute-done.12.refs_11_), channel_id=1, source_target_pairs={{0,4},{1,5},{2,6},{3,7},{4,8},{5,9},{6,10},{7,11},{8,12},{9,13},{1... | collective-permute-start | bytes 1179656 | tf_op jit(solution)/shard_map/ppermute | solution.py:32
  111.7 14.4 %collective-permute-start.29 = (bf16[5,2,64,384]{3,2,1,0:T(8,128)(2,1)}, bf16[5,2,64,384]{3,2,1,0:T(8,128)(2,1)S(1)}, u32[]{:S(2)}, u32[]{:S(2)}) collective-permute-start(bf16[5,2,64,384]{3,2,1,0:T(8,128)(2,1)} %collective-permute-done.27.refs_21_), channel_id=1, source_target_pairs={{0,96},{1,97},{2,98},{3,99},{4,100},{5,101},{6,102},{7,103},{8,104... | collective-permute-start | bytes 1474568 | tf_op jit(solution)/shard_map/ppermute | solution.py:32
  114.6 11.5 %collective-permute-start.15 = (bf16[4,2,64,384]{3,2,1,0:T(8,128)(2,1)}, bf16[4,2,64,384]{3,2,1,0:T(8,128)(2,1)S(1)}, u32[]{:S(2)}, u32[]{:S(2)}) collective-permute-start(bf16[4,2,64,384]{3,2,1,0:T(8,128)(2,1)} %collective-permute-done.13.refs_12_), channel_id=1, source_target_pairs={{0,28},{1,29},{2,30},{3,31},{4,0},{5,1},{6,2},{7,3},{8,4},{9,5},{1... | collective-permute-start | bytes 1179656 | tf_op jit(solution)/shard_map/ppermute | solution.py:32
  122.4 11.8 %collective-permute-start.16 = (bf16[4,2,64,384]{3,2,1,0:T(8,128)(2,1)S(1)}, bf16[4,2,64,384]{3,2,1,0:T(8,128)(2,1)S(1)}, u32[]{:S(2)}, u32[]{:S(2)}) collective-permute-start(bf16[4,2,64,384]{3,2,1,0:T(8,128)(2,1)S(1)} %collective-permute-done.14.refs_13_), channel_id=1, source_target_pairs={{0,4},{1,5},{2,6},{3,7},{4,8},{5,9},{6,10},{7,11},{8,12},{9,13},{1... | collective-permute-start | bytes 1179656 | tf_op jit(solution)/shard_map/ppermute | solution.py:32
  165.1 28.1 %all-to-all-start = ((bf16[256,2,256]{2,1,0:T(2,128)(2,1)}), bf16[256,2,256]{2,1,0:T(2,128)(2,1)S(1)}, u32[]{:S(2)}, u32[]{:S(2)}) async-start(bf16[256,2,256]{2,1,0:T(2,128)(2,1)} %reshape.40), calls=%async_computation | async-start | bytes 524288 | tf_op jit(solution)/shard_map/all_to_all | solution.py:458
  178.3 22.0 %collective-permute-start.34 = (bf16[2,256,512]{2,1,0:T(8,128)(2,1)}, bf16[2,256,512]{2,1,0:T(8,128)(2,1)S(1)}, u32[]{:S(2)}, u32[]{:S(2)}) collective-permute-start(bf16[2,256,512]{2,1,0:T(8,128)(2,1)} %get-tuple-element.22), channel_id=1, source_target_pairs={{0,2},{1,3},{2,0},{3,1},{4,6},{5,7},{6,4},{7,5},{8,10},{9,11},{10,... | collective-permute-start | bytes 1572872 | tf_op jit(solution)/shard_map/ppermute | solution.py:32
  194.4 19.1 %all-to-all-start.1 = ((bf16[64,2,1024]{2,1,0:T(2,128)(2,1)}), bf16[64,2,1024]{2,1,0:T(2,128)(2,1)S(1)}, u32[]{:S(2)}, u32[]{:S(2)}) async-start(bf16[64,2,1024]{2,1,0:T(2,128)(2,1)} %broadcast_in_dim.2), calls=%async_computation.1 | async-start | bytes 524288 | tf_op jit(solution)/shard_map/all_to_all | solution.py:57
  200.3 14.7 %collective-permute-start.35 = (bf16[2,256,512]{2,1,0:T(8,128)(2,1)S(1)}, bf16[2,256,512]{2,1,0:T(8,128)(2,1)S(1)}, u32[]{:S(2)}, u32[]{:S(2)}) collective-permute-start(bf16[2,256,512]{2,1,0:T(8,128)(2,1)S(1)} %collective-permute-done.34.refs_2_), channel_id=1, source_target_pairs={{0,1},{1,0},{2,3},{3,2},{4,5},{5,4},{6,7},{7,6},{8,9},{9,8},{10,11... | collective-permute-start | bytes 1572872 | tf_op jit(solution)/shard_map/ppermute | solution.py:32
  200.4 14.6 %collective-permute-start.33 = (bf16[256,512]{1,0:T(8,128)(2,1)}, bf16[256,512]{1,0:T(8,128)(2,1)}, u32[]{:S(2)}, u32[]{:S(2)}) collective-permute-start(bf16[256,512]{1,0:T(8,128)(2,1)} %get-tuple-element.21), channel_id=1, source_target_pairs={{0,1},{1,0},{2,3},{3,2},{4,5},{5,4},{6,7},{7,6},{8,9},{9,8},{10,11... | collective-permute-start | bytes 786440 | tf_op jit(solution)/shard_map/ppermute | solution.py:32
  (30 other events, 504.7 us)
where the time goes:
time: 221 us; the launch traced here: 219 us
  waiting for transfers between devices  99 us (45%)
  starting transfers between devices  62.5 us (28%)
  Pallas kernels  39.3 us (18%)
  local copies, waits for them, and re-layouts  13.7 us (6%)
  other arithmetic  3.14 us (1%)
    ppermute x36, waiting for transfers between devices, permute(): return lax.ppermute(value, MESH_AXES, pairs)  73.1 us
    ppermute x36, starting transfers between devices, permute(): return lax.ppermute(value, MESH_AXES, pairs)  43.4 us
    pallas_call x1, Pallas kernels, layer(): pl.pallas_call(layer_kernel, grid_spec=pltpu.PrefetchScalarGridSpec(num_s...  26.9 us
    all_to_all x1, waiting for transfers between devices, layer_step(): lax.all_to_all(gradient.reshape(256, 2, 256), ('owner', 'fsdp', 'dp'), 0,...  13.3 us
    all_to_all x1, starting transfers between devices, layer_step(): lax.all_to_all(gradient.reshape(256, 2, 256), ('owner', 'fsdp', 'dp'), 0,...  13.2 us
    all_to_all x1, waiting for transfers between devices, spread(): return lax.all_to_all(copies, axes, 0, 0, tiled=True)  12.6 us
    unnamed x52, local copies, waits for them, and re-layouts  7.81 us
    all_to_all x1, starting transfers between devices, spread(): return lax.all_to_all(copies, axes, 0, 0, tiled=True)  5.86 us
  transfers between devices with their start and end apart: 38, of which 17 were waited for; matrix products, arithmetic and copies ran while one was open for 4% of the time, Pallas kernels for 4%

commit v1 on v0

--- a/solution.py
+++ b/solution.py
@@ -166,7 +166,7 @@
     x_pieces = refs[16:24]
     packed, cosine, sine = refs[24:28], refs[28], refs[29]
     outs, gradient = refs[30:33], refs[33]
-    weights, rows, keys, values, ups, out, sums, piece_sem, row_sem, up_sem = refs[34:]
+    weights, rows, keys, values, ups, out, sums, heads, piece_sem, row_sem, up_sem = refs[34:]
     step = pl.program_id(0)
     y_hi, x, z = place[1], place[2], place[3]
 
@@ -196,12 +196,11 @@
         return copies
 
     def row_copies(index):
-        slot = index % 2
         return [
             pltpu.make_async_copy(
                 states[2 * index + half],
-                rows.at[slot, pl.ds(half * 128, 128)],
-                row_sem.at[slot, half],
+                rows.at[index, pl.ds(half * 128, 128)],
+                row_sem.at[index, half],
             )
             for half in range(2)
         ]
@@ -214,15 +213,49 @@
             )
         ]
 
+    def load(first):
+        for index in (first, first + 1):
+            for copy in row_copies(index):
+                copy.wait()
+
     @pl.when(step == 0)
     def _():
-        for copy in piece_copies():
+        copies = piece_copies()
+        for copy in copies[:32] + row_copies(0) + row_copies(1) + copies[32:]:
             copy.start()
-        for copy in row_copies(0) + row_copies(1):
-            copy.start()
-        for copy in up_copies():
+        for copy in up_copies() + row_copies(2) + row_copies(3):
             copy.start()
         sums[...] = jnp.zeros_like(sums)
+        load(0)
+        for copy in copies:
+            copy.wait()
+
+    @pl.when(step == 2)
+    def _():
+        load(2)
+
+    @pl.when(lax.rem(step, 2) == 0)
+    def _():
+        def project(block, carry):
+            columns = pl.ds(pl.multiple_of(block * 256, 256), 256)
+            both = sum(
+                dot(
+                    rows[
+                        pl.ds(step, 2), :, pl.ds(pl.multiple_of((y_hi ^ side) * 2048, 2048), 2048)
+                    ].reshape(2 * ROWS, 2048),
+                    weights[side, :, :, :, columns].reshape(2048, 256),
+                    1,
+                    0,
+                )
+                for side in range(2)
+            )
+            heads[:, :, columns] = both.reshape(2, ROWS, 256)
+            return carry
+
+        lax.fori_loop(0, 3, project, 0)
+
+    @pl.when(step == 0)
+    def _():
         for copy in up_copies():
             copy.wait()
         for index in range(4):
@@ -231,43 +264,22 @@
                 target = pl.ds(first + half * 64, 64)
                 keys[target, :] = ups[index, ROWS:, half * 128 : half * 128 + 128]
                 values[target, :] = ups[index, ROWS:, 256 + half * 128 : 384 + half * 128]
-        for copy in piece_copies():
-            copy.wait()
-
-    for index in range(4):
-
-        @pl.when(step == index)
-        def _():
-            if index in (1, 2):
-                for copy in row_copies(index + 1):
-                    copy.start()
-            for copy in row_copies(index):
-                copy.wait()
-
-    slot = lax.rem(step, 2)
-    projected = sum(
-        dot(
-            rows[slot, :, pl.ds(pl.multiple_of((y_hi ^ side) * 2048, 2048), 2048)],
-            weights[side].reshape(2048, COLS),
-            1,
-            0,
-        )
-        for side in range(2)
-    )
+
+    which = lax.rem(step, 2)
     cos, sin = cosine[...], sine[...]
 
     def rope(v):
         return (v * cos + pltpu.roll(v, HEAD_SIZE // 2, 1) * sin).astype(jnp.bfloat16)
 
-    own_keys = rope(projected[:, 512:640])
-    own_values = projected[:, 640:768].astype(jnp.bfloat16)
+    own_keys = rope(heads[which, :, 512:640])
+    own_values = heads[which, :, 640:768].astype(jnp.bfloat16)
     prefix_keys, prefix_values = keys[...], values[...]
     causal = lax.broadcasted_iota(jnp.int32, (ROWS, ROWS), 0) >= lax.broadcasted_iota(
         jnp.int32, (ROWS, ROWS), 1
     )
     scale = HEAD_SIZE ** (-0.5) * LOG2E
     lanes = [slice(h * HEAD_SIZE, (h + 1) * HEAD_SIZE) for h in range(GROUP)]
-    queries = [rope(projected[:, lane]) for lane in lanes]
+    queries = [rope(heads[which, :, lane]) for lane in lanes]
     key_sum = jnp.zeros((HEAD_SIZE, PREFIX), jnp.float32)
     value_sum = jnp.zeros((HEAD_SIZE, PREFIX), jnp.float32)
 
@@ -354,14 +366,15 @@
             ],
             scratch_shapes=[
                 pltpu.VMEM((2, X_SIZE, Z_SIZE, 64, COLS), jnp.bfloat16),
-                pltpu.VMEM((2, ROWS, WIDTH), jnp.bfloat16),
+                pltpu.VMEM((4, ROWS, WIDTH), jnp.bfloat16),
                 pltpu.VMEM((PREFIX, HEAD_SIZE), jnp.bfloat16),
                 pltpu.VMEM((PREFIX, HEAD_SIZE), jnp.bfloat16),
                 pltpu.VMEM((4, 320, 512), jnp.bfloat16),
                 pltpu.VMEM((ROWS, 512), jnp.bfloat16),
                 pltpu.VMEM((256, PREFIX), jnp.float32),
+                pltpu.VMEM((2, ROWS, COLS), jnp.float32),
                 pltpu.SemaphoreType.DMA((64,)),
-                pltpu.SemaphoreType.DMA((2, 2)),
+                pltpu.SemaphoreType.DMA((4, 2)),
                 pltpu.SemaphoreType.DMA((4,)),
             ],
         ),

time: 221 us -> 219 us (level)
  no operation moved by 1% of the time
where the time goes in v1:
time: 219 us; the launch traced here: 217 us
  waiting for transfers between devices  99 us (45%)
  starting transfers between devices  62.5 us (29%)
  Pallas kernels  37.4 us (17%)
  local copies, waits for them, and re-layouts  13.7 us (6%)
  other arithmetic  3.14 us (1%)
    ppermute x36, waiting for transfers between devices, permute(): return lax.ppermute(value, MESH_AXES, pairs)  73.1 us
    ppermute x36, starting transfers between devices, permute(): return lax.ppermute(value, MESH_AXES, pairs)  43.4 us
    pallas_call x1, Pallas kernels, layer(): pl.pallas_call(layer_kernel, grid_spec=pltpu.PrefetchScalarGridSpec(num_s...  25 us
    all_to_all x1, waiting for transfers between devices, layer_step(): lax.all_to_all(gradient.reshape(256, 2, 256), ('owner', 'fsdp', 'dp'), 0,...  13.3 us
    all_to_all x1, starting transfers between devices, layer_step(): lax.all_to_all(gradient.reshape(256, 2, 256), ('owner', 'fsdp', 'dp'), 0,...  13.2 us
    all_to_all x1, waiting for transfers between devices, spread(): return lax.all_to_all(copies, axes, 0, 0, tiled=True)  12.6 us
    unnamed x52, local copies, waits for them, and re-layouts  7.81 us
    all_to_all x1, starting transfers between devices, spread(): return lax.all_to_all(copies, axes, 0, 0, tiled=True)  5.86 us
  transfers between devices with their start and end apart: 38, of which 17 were waited for; matrix products, arithmetic and copies ran while one was open for 4% of the time, Pallas kernels for 4%

profile of v1, /device:TPU:2, one launch (start us, length us, event | category | flops | bytes accessed | tf_op | source)
XLA Modules:
  0.0 217.4 jit_solution(11879736846089576657)
XLA Ops:
  2.4 3.1 %collective-permute-start.6 = (bf16[64,768]{1,0:T(8,128)(2,1)S(1)}, bf16[64,768]{1,0:T(8,128)(2,1)S(1)}, u32[]{:S(2)}, u32[]{:S(2)}) collective-permute-start(bf16[64,768]{1,0:T(8,128)(2,1)S(1)} %get-tuple-element.16), channel_id=1, source_target_pairs={{0,130},{1,131},{2,128},{3,129},{4,134},{5,135},{6,132},{7,133},{8... | collective-permute-start | bytes 294920 | tf_op jit(solution)/shard_map/ppermute | solution.py:32
  5.5 2.8 %collective-permute-done.6 = bf16[64,768]{1,0:T(8,128)(2,1)S(1)} collective-permute-done((bf16[64,768]{1,0:T(8,128)(2,1)S(1)}, bf16[64,768]{1,0:T(8,128)(2,1)S(1)}, u32[]{:S(2)}, u32[]{:S(2)}) %collective-permute-start.6) | collective-permute-done | bytes 98336 | tf_op jit(solution)/shard_map/ppermute | solution.py:32
  8.3 2.0 collective-permute-start.17
  10.3 4.0 %collective-permute-start.18 = (bf16[2,64,384]{2,1,0:T(8,128)(2,1)S(1)}, bf16[2,64,384]{2,1,0:T(8,128)(2,1)S(1)}, u32[]{:S(2)}, u32[]{:S(2)}) collective-permute-start(bf16[2,64,384]{2,1,0:T(8,128)(2,1)S(1)} %get-tuple-element.29), channel_id=1, source_target_pairs={{0,28},{1,29},{2,30},{3,31},{4,0},{5,1},{6,2},{7,3},{8,4},{9,5},{1... | collective-permute-start | bytes 294920 | tf_op jit(solution)/shard_map/ppermute | solution.py:32
  15.6 4.0 %shard_map.122 = (bf16[320,512]{1,0:T(8,128)(2,1)}, bf16[320,512]{1,0:T(8,128)(2,1)}, bf16[2,320,512]{2,1,0:T(8,128)(2,1)}) custom-call(s32[5]{0:T(128)} %stack.73.place, bf16[1,256,2048]{2,1,0:T(8,128)(2,1)} %cotangent.1, f32[128,1024]{1,0:T(8,128)} %value_rows.1, f32[128,1024]{1,0:T(8,128)} %value_rows.1), custom_call_target="tpu_custom_call" | custom-call | tf_op jit(solution)/shard_map/pallas_call | solution.py:119
  20.5 2.4 %collective-permute-start.8 = (bf16[2,64,384]{2,1,0:T(8,128)(2,1)S(1)}, bf16[2,64,384]{2,1,0:T(8,128)(2,1)S(1)}, u32[]{:S(2)}, u32[]{:S(2)}) collective-permute-start(bf16[2,64,384]{2,1,0:T(8,128)(2,1)S(1)} %get-tuple-element.30), channel_id=1, source_target_pairs={{0,64},{1,65},{2,66},{3,67},{4,68},{5,69},{6,70},{7,71},{8,72},{9,... | collective-permute-start | bytes 294920 | tf_op jit(solution)/shard_map/ppermute | solution.py:32
  24.9 2.2 %collective-permute-start.24 = (bf16[3,2,64,384]{3,2,1,0:T(8,128)(2,1)S(1)}, bf16[3,2,64,384]{3,2,1,0:T(8,128)(2,1)}, u32[]{:S(2)}, u32[]{:S(2)}) collective-permute-start(bf16[3,2,64,384]{3,2,1,0:T(8,128)(2,1)S(1)} %pad_maximum_fusion.1.refs_16_), channel_id=1, source_target_pairs={{0,32},{1,33},{2,34},{3,35},{4,36},{5,37},{6,38},{7,39},{8,40},{9,... | collective-permute-start | bytes 884744 | tf_op jit(solution)/shard_map/ppermute | solution.py:32
  29.8 2.0 collective-permute-start.11
  31.8 2.0 collective-permute-done.19
  35.1 6.1 %collective-permute-done.20 = bf16[2,64,384]{2,1,0:T(8,128)(2,1)S(1)} collective-permute-done((bf16[2,64,384]{2,1,0:T(8,128)(2,1)S(1)}, bf16[2,64,384]{2,1,0:T(8,128)(2,1)S(1)}, u32[]{:S(2)}, u32[]{:S(2)}) %collective-permute-start.20) | collective-permute-done | bytes 98336 | tf_op jit(solution)/shard_map/ppermute | solution.py:32
  42.2 3.2 %collective-permute-start.22 = (bf16[2,64,384]{2,1,0:T(8,128)(2,1)S(1)}, bf16[2,64,384]{2,1,0:T(8,128)(2,1)S(1)}, u32[]{:S(2)}, u32[]{:S(2)}) collective-permute-start(bf16[2,64,384]{2,1,0:T(8,128)(2,1)S(1)} %collective-permute-done.20), channel_id=1, source_target_pairs={{0,28},{1,29},{2,30},{3,31},{4,0},{5,1},{6,2},{7,3},{8,4},{9,5},{1... | collective-permute-start | bytes 294920 | tf_op jit(solution)/shard_map/ppermute | solution.py:32
  45.4 1.9 collective-permute-done.21
  48.0 3.2 %collective-permute-start.26 = (bf16[3,2,64,384]{3,2,1,0:T(8,128)(2,1)S(1)}, bf16[3,2,64,384]{3,2,1,0:T(8,128)(2,1)S(1)}, u32[]{:S(2)}, u32[]{:S(2)}) collective-permute-start(bf16[3,2,64,384]{3,2,1,0:T(8,128)(2,1)S(1)} %pad_maximum_fusion.1.refs_16_), channel_id=1, source_target_pairs={{0,96},{1,97},{2,98},{3,99},{4,100},{5,101},{6,102},{7,103},{8,104... | collective-permute-start | bytes 884744 | tf_op jit(solution)/shard_map/ppermute | solution.py:32
  51.2 2.4 %collective-permute-done.23 = bf16[2,64,384]{2,1,0:T(8,128)(2,1)S(1)} collective-permute-done((bf16[2,64,384]{2,1,0:T(8,128)(2,1)S(1)}, bf16[2,64,384]{2,1,0:T(8,128)(2,1)S(1)}, u32[]{:S(2)}, u32[]{:S(2)}) %collective-permute-start.23) | collective-permute-done | bytes 98336 | tf_op jit(solution)/shard_map/ppermute | solution.py:32
  54.3 2.7 %collective-permute-start.28 = (bf16[3,2,64,384]{3,2,1,0:T(8,128)(2,1)}, bf16[3,2,64,384]{3,2,1,0:T(8,128)(2,1)}, u32[]{:S(2)}, u32[]{:S(2)}) collective-permute-start(bf16[3,2,64,384]{3,2,1,0:T(8,128)(2,1)} %collective-permute-done.24.refs_18_), channel_id=1, source_target_pairs={{0,32},{1,33},{2,34},{3,35},{4,36},{5,37},{6,38},{7,39},{8,40},{9,... | collective-permute-start | bytes 884744 | tf_op jit(solution)/shard_map/ppermute | solution.py:32
  57.0 3.1 %collective-permute-start.13 = (bf16[4,2,64,384]{3,2,1,0:T(8,128)(2,1)S(1)}, bf16[4,2,64,384]{3,2,1,0:T(8,128)(2,1)}, u32[]{:S(2)}, u32[]{:S(2)}) collective-permute-start(bf16[4,2,64,384]{3,2,1,0:T(8,128)(2,1)S(1)} %collective-permute-done.11.refs_10_), channel_id=1, source_target_pairs={{0,28},{1,29},{2,30},{3,31},{4,0},{5,1},{6,2},{7,3},{8,4},{9,5},{1... | collective-permute-start | bytes 1179656 | tf_op jit(solution)/shard_map/ppermute | solution.py:32
  61.4 2.4 %shard_map.121.refs_1_ = bf16[128,4096]{1,0:T(8,128)(2,1)} custom-call(bf16[1,256,4096]{2,1,0:T(8,128)(2,1)} %states.1, f32[1,4096]{1,0:T(1,128)} %bitcast.34), custom_call_target="tpu_custom_call" | custom-call | tf_op jit(solution)/shard_map/pallas_call | solution.py:85
  63.8 2.5 %shard_map.120.refs_0_ = bf16[128,4096]{1,0:T(8,128)(2,1)} custom-call(bf16[1,256,4096]{2,1,0:T(8,128)(2,1)} %states.1, f32[1,4096]{1,0:T(1,128)} %bitcast.35), custom_call_target="tpu_custom_call" | custom-call | tf_op jit(solution)/shard_map/pallas_call | solution.py:85
  68.6 9.1 %collective-permute-done.12.refs_11_ = bf16[4,2,64,384]{3,2,1,0:T(8,128)(2,1)S(1)} collective-permute-done((bf16[4,2,64,384]{3,2,1,0:T(8,128)(2,1)}, bf16[4,2,64,384]{3,2,1,0:T(8,128)(2,1)S(1)}, u32[]{:S(2)}, u32[]{:S(2)}) %collective-permute-start.12) | collective-permute-done | bytes 393248 | tf_op jit(solution)/shard_map/ppermute | solution.py:32
  79.1 13.5 %collective-permute-done.25.refs_19_ = bf16[5,2,64,384]{3,2,1,0:T(8,128)(2,1)S(1)} collective-permute-done((bf16[5,2,64,384]{3,2,1,0:T(8,128)(2,1)}, bf16[5,2,64,384]{3,2,1,0:T(8,128)(2,1)S(1)}, u32[]{:S(2)}, u32[]{:S(2)}) %collective-permute-start.25) | collective-permute-done | bytes 491552 | tf_op jit(solution)/shard_map/ppermute | solution.py:32
  93.1 16.6 %collective-permute-done.3.refs_5_ = bf16[128,4096]{1,0:T(8,128)(2,1)S(1)} collective-permute-done((bf16[128,4096]{1,0:T(8,128)(2,1)S(1)}, bf16[128,4096]{1,0:T(8,128)(2,1)S(1)}, u32[]{:S(2)}, u32[]{:S(2)}) %collective-permute-start.3) | collective-permute-done | bytes 1048608 | tf_op jit(solution)/shard_map/ppermute | solution.py:32
  111.7 2.9 %collective-permute-start.29 = (bf16[5,2,64,384]{3,2,1,0:T(8,128)(2,1)}, bf16[5,2,64,384]{3,2,1,0:T(8,128)(2,1)S(1)}, u32[]{:S(2)}, u32[]{:S(2)}) collective-permute-start(bf16[5,2,64,384]{3,2,1,0:T(8,128)(2,1)} %collective-permute-done.27.refs_21_), channel_id=1, source_target_pairs={{0,96},{1,97},{2,98},{3,99},{4,100},{5,101},{6,102},{7,103},{8,104... | collective-permute-start | bytes 1474568 | tf_op jit(solution)/shard_map/ppermute | solution.py:32
  114.6 2.4 %collective-permute-start.15 = (bf16[4,2,64,384]{3,2,1,0:T(8,128)(2,1)}, bf16[4,2,64,384]{3,2,1,0:T(8,128)(2,1)S(1)}, u32[]{:S(2)}, u32[]{:S(2)}) collective-permute-start(bf16[4,2,64,384]{3,2,1,0:T(8,128)(2,1)} %collective-permute-done.13.refs_12_), channel_id=1, source_target_pairs={{0,28},{1,29},{2,30},{3,31},{4,0},{5,1},{6,2},{7,3},{8,4},{9,5},{1... | collective-permute-start | bytes 1179656 | tf_op jit(solution)/shard_map/ppermute | solution.py:32
  117.0 5.5 %collective-permute-done.14.refs_13_ = bf16[4,2,64,384]{3,2,1,0:T(8,128)(2,1)S(1)} collective-permute-done((bf16[4,2,64,384]{3,2,1,0:T(8,128)(2,1)S(1)}, bf16[4,2,64,384]{3,2,1,0:T(8,128)(2,1)S(1)}, u32[]{:S(2)}, u32[]{:S(2)}) %collective-permute-start.14) | collective-permute-done | bytes 393248 | tf_op jit(solution)/shard_map/ppermute | solution.py:32
  123.9 2.2 %collective-permute-done.15.refs_14_ = bf16[4,2,64,384]{3,2,1,0:T(8,128)(2,1)S(1)} collective-permute-done((bf16[4,2,64,384]{3,2,1,0:T(8,128)(2,1)}, bf16[4,2,64,384]{3,2,1,0:T(8,128)(2,1)S(1)}, u32[]{:S(2)}, u32[]{:S(2)}) %collective-permute-start.15) | collective-permute-done | bytes 393248 | tf_op jit(solution)/shard_map/ppermute | solution.py:32
  126.1 8.1 %collective-permute-done.16.refs_15_ = bf16[4,2,64,384]{3,2,1,0:T(8,128)(2,1)S(1)} collective-permute-done((bf16[4,2,64,384]{3,2,1,0:T(8,128)(2,1)S(1)}, bf16[4,2,64,384]{3,2,1,0:T(8,128)(2,1)S(1)}, u32[]{:S(2)}, u32[]{:S(2)}) %collective-permute-start.16) | collective-permute-done | bytes 393248 | tf_op jit(solution)/shard_map/ppermute | solution.py:32
  136.3 25.0 %shard_map.123 = (bf16[256,512]{1,0:T(8,128)(2,1)}, bf16[256,512]{1,0:T(8,128)(2,1)}, bf16[2,256,512]{2,1,0:T(8,128)(2,1)}, bf16[512,256]{1,0:T(8,128)(2,1)}) custom-call(s32[5]{0:T(128)} %stack.73.place, bf16[128,4096]{1,0:T(8,128)(2,1)} %shard_map.120.refs_0_, bf16[128,4096]{1,0:T(8,128)(2,1)} %shard_map.121.refs_1_, bf16[128,4096]{1,0:T(8,128)(2,1)} %copy-done.6, ...), custom_call_target="tpu_custom_call" | custom-call | tf_op jit(solution)/shard_map/pallas_call | solution.py:356
  163.2 13.2 %all-to-all-start = ((bf16[256,2,256]{2,1,0:T(2,128)(2,1)}), bf16[256,2,256]{2,1,0:T(2,128)(2,1)S(1)}, u32[]{:S(2)}, u32[]{:S(2)}) async-start(bf16[256,2,256]{2,1,0:T(2,128)(2,1)} %reshape.40), calls=%async_computation | async-start | bytes 524288 | tf_op jit(solution)/shard_map/all_to_all | solution.py:471
  178.0 13.3 %all-to-all-done = bf16[256,2,256]{2,1,0:T(2,128)(2,1)S(1)} async-done(((bf16[256,2,256]{2,1,0:T(2,128)(2,1)}), bf16[256,2,256]{2,1,0:T(2,128)(2,1)S(1)}, u32[]{:S(2)}, u32[]{:S(2)}) %all-to-all-start) | async-done | bytes 262176 | tf_op jit(solution)/shard_map/all_to_all | solution.py:471
  192.5 5.9 %all-to-all-start.1 = ((bf16[64,2,1024]{2,1,0:T(2,128)(2,1)}), bf16[64,2,1024]{2,1,0:T(2,128)(2,1)S(1)}, u32[]{:S(2)}, u32[]{:S(2)}) async-start(bf16[64,2,1024]{2,1,0:T(2,128)(2,1)} %broadcast_in_dim.2), calls=%async_computation.1 | async-start | bytes 524288 | tf_op jit(solution)/shard_map/all_to_all | solution.py:57
  199.0 12.6 %all-to-all-done.1 = bf16[64,2,1024]{2,1,0:T(2,128)(2,1)S(1)} async-done(((bf16[64,2,1024]{2,1,0:T(2,128)(2,1)}), bf16[64,2,1024]{2,1,0:T(2,128)(2,1)S(1)}, u32[]{:S(2)}, u32[]{:S(2)}) %all-to-all-start.1) | async-done | bytes 262176 | tf_op jit(solution)/shard_map/all_to_all | solution.py:57
  213.9 3.5 %shard_map.124 = bf16[1,256,2048]{2,1,0:T(8,128)(2,1)} custom-call(s32[5]{0:T(128)} %stack.73.place, bf16[256,512]{1,0:T(8,128)(2,1)} %get-tuple-element.20.refs_0_, bf16[256,512]{1,0:T(8,128)(2,1)} %collective-permute-done.33.refs_1_, bf16[2,256,512]{2,1,0:T(8,128)(2,1)} %copy-done.13, bf16[2,256,512]{2,1,0:T(8,128)(2,1)} %copy-done.14), custom_call_target="tpu_custom_call" | custom-call | tf_op jit(solution)/shard_map/pallas_call | solution.py:147
  (121 shorter events, 29.9 us)
Async XLA Ops:
  8.3 12.2 %collective-permute-start.17 = (bf16[2,64,384]{2,1,0:T(8,128)(2,1)S(1)}, bf16[2,64,384]{2,1,0:T(8,128)(2,1)S(1)}, u32[]{:S(2)}, u32[]{:S(2)}) collective-permute-start(bf16[2,64,384]{2,1,0:T(8,128)(2,1)S(1)} %get-tuple-element.29), channel_id=1, source_target_pairs={{0,4},{1,5},{2,6},{3,7},{4,8},{5,9},{6,10},{7,11},{8,12},{9,13},{1... | collective-permute-start | bytes 294920 | tf_op jit(solution)/shard_map/ppermute | solution.py:32
  10.3 12.7 %collective-permute-start.18 = (bf16[2,64,384]{2,1,0:T(8,128)(2,1)S(1)}, bf16[2,64,384]{2,1,0:T(8,128)(2,1)S(1)}, u32[]{:S(2)}, u32[]{:S(2)}) collective-permute-start(bf16[2,64,384]{2,1,0:T(8,128)(2,1)S(1)} %get-tuple-element.29), channel_id=1, source_target_pairs={{0,28},{1,29},{2,30},{3,31},{4,0},{5,1},{6,2},{7,3},{8,4},{9,5},{1... | collective-permute-start | bytes 294920 | tf_op jit(solution)/shard_map/ppermute | solution.py:32
  19.6 22.6 %collective-permute-start.30 = (bf16[320,512]{1,0:T(8,128)(2,1)}, bf16[320,512]{1,0:T(8,128)(2,1)S(1)}, u32[]{:S(2)}, u32[]{:S(2)}) collective-permute-start(bf16[320,512]{1,0:T(8,128)(2,1)} %get-tuple-element.18), channel_id=1, source_target_pairs={{0,1},{1,0},{2,3},{3,2},{4,5},{5,4},{6,7},{7,6},{8,9},{9,8},{10,11... | collective-permute-start | bytes 983048 | tf_op jit(solution)/shard_map/ppermute | solution.py:32
  19.6 48.5 %collective-permute-start.31 = (bf16[2,320,512]{2,1,0:T(8,128)(2,1)}, bf16[2,320,512]{2,1,0:T(8,128)(2,1)}, u32[]{:S(2)}, u32[]{:S(2)}) collective-permute-start(bf16[2,320,512]{2,1,0:T(8,128)(2,1)} %get-tuple-element.19), channel_id=1, source_target_pairs={{0,2},{1,3},{2,0},{3,1},{4,6},{5,7},{6,4},{7,5},{8,10},{9,11},{10,... | collective-permute-start | bytes 1966088 | tf_op jit(solution)/shard_map/ppermute | solution.py:32
  20.5 7.4 %collective-permute-start.8 = (bf16[2,64,384]{2,1,0:T(8,128)(2,1)S(1)}, bf16[2,64,384]{2,1,0:T(8,128)(2,1)S(1)}, u32[]{:S(2)}, u32[]{:S(2)}) collective-permute-start(bf16[2,64,384]{2,1,0:T(8,128)(2,1)S(1)} %get-tuple-element.30), channel_id=1, source_target_pairs={{0,64},{1,65},{2,66},{3,67},{4,68},{5,69},{6,70},{7,71},{8,72},{9,... | collective-permute-start | bytes 294920 | tf_op jit(solution)/shard_map/ppermute | solution.py:32
  22.9 6.8 %collective-permute-start.7 = (bf16[2,64,384]{2,1,0:T(8,128)(2,1)S(1)}, bf16[2,64,384]{2,1,0:T(8,128)(2,1)S(1)}, u32[]{:S(2)}, u32[]{:S(2)}) collective-permute-start(bf16[2,64,384]{2,1,0:T(8,128)(2,1)S(1)} %get-tuple-element.30), channel_id=1, source_target_pairs={{0,32},{1,33},{2,34},{3,35},{4,36},{5,37},{6,38},{7,39},{8,40},{9,... | collective-permute-start | bytes 294920 | tf_op jit(solution)/shard_map/ppermute | solution.py:32
  24.9 29.4 %collective-permute-start.24 = (bf16[3,2,64,384]{3,2,1,0:T(8,128)(2,1)S(1)}, bf16[3,2,64,384]{3,2,1,0:T(8,128)(2,1)}, u32[]{:S(2)}, u32[]{:S(2)}) collective-permute-start(bf16[3,2,64,384]{3,2,1,0:T(8,128)(2,1)S(1)} %pad_maximum_fusion.1.refs_16_), channel_id=1, source_target_pairs={{0,32},{1,33},{2,34},{3,35},{4,36},{5,37},{6,38},{7,39},{8,40},{9,... | collective-permute-start | bytes 884744 | tf_op jit(solution)/shard_map/ppermute | solution.py:32
  29.8 27.2 %collective-permute-start.11 = (bf16[4,2,64,384]{3,2,1,0:T(8,128)(2,1)S(1)}, bf16[4,2,64,384]{3,2,1,0:T(8,128)(2,1)S(1)}, u32[]{:S(2)}, u32[]{:S(2)}) collective-permute-start(bf16[4,2,64,384]{3,2,1,0:T(8,128)(2,1)S(1)} %pad_maximum_fusion.refs_8_), channel_id=1, source_target_pairs={{0,28},{1,29},{2,30},{3,31},{4,0},{5,1},{6,2},{7,3},{8,4},{9,5},{1... | collective-permute-start | bytes 1179656 | tf_op jit(solution)/shard_map/ppermute | solution.py:32
  33.8 7.5 %collective-permute-start.20 = (bf16[2,64,384]{2,1,0:T(8,128)(2,1)S(1)}, bf16[2,64,384]{2,1,0:T(8,128)(2,1)S(1)}, u32[]{:S(2)}, u32[]{:S(2)}) collective-permute-start(bf16[2,64,384]{2,1,0:T(8,128)(2,1)S(1)} %collective-permute-done.18), channel_id=1, source_target_pairs={{0,28},{1,29},{2,30},{3,31},{4,0},{5,1},{6,2},{7,3},{8,4},{9,5},{1... | collective-permute-start | bytes 294920 | tf_op jit(solution)/shard_map/ppermute | solution.py:32
  48.0 12.7 %collective-permute-start.26 = (bf16[3,2,64,384]{3,2,1,0:T(8,128)(2,1)S(1)}, bf16[3,2,64,384]{3,2,1,0:T(8,128)(2,1)S(1)}, u32[]{:S(2)}, u32[]{:S(2)}) collective-permute-start(bf16[3,2,64,384]{3,2,1,0:T(8,128)(2,1)S(1)} %pad_maximum_fusion.1.refs_16_), channel_id=1, source_target_pairs={{0,96},{1,97},{2,98},{3,99},{4,100},{5,101},{6,102},{7,103},{8,104... | collective-permute-start | bytes 884744 | tf_op jit(solution)/shard_map/ppermute | solution.py:32
  53.6 12.7 %collective-permute-start.10 = (bf16[4,2,64,384]{3,2,1,0:T(8,128)(2,1)S(1)}, bf16[4,2,64,384]{3,2,1,0:T(8,128)(2,1)}, u32[]{:S(2)}, u32[]{:S(2)}) collective-permute-start(bf16[4,2,64,384]{3,2,1,0:T(8,128)(2,1)S(1)} %pad_maximum_fusion.refs_8_), channel_id=1, source_target_pairs={{0,4},{1,5},{2,6},{3,7},{4,8},{5,9},{6,10},{7,11},{8,12},{9,13},{1... | collective-permute-start | bytes 1179656 | tf_op jit(solution)/shard_map/ppermute | solution.py:32
  54.3 14.2 %collective-permute-start.28 = (bf16[3,2,64,384]{3,2,1,0:T(8,128)(2,1)}, bf16[3,2,64,384]{3,2,1,0:T(8,128)(2,1)}, u32[]{:S(2)}, u32[]{:S(2)}) collective-permute-start(bf16[3,2,64,384]{3,2,1,0:T(8,128)(2,1)} %collective-permute-done.24.refs_18_), channel_id=1, source_target_pairs={{0,32},{1,33},{2,34},{3,35},{4,36},{5,37},{6,38},{7,39},{8,40},{9,... | collective-permute-start | bytes 884744 | tf_op jit(solution)/shard_map/ppermute | solution.py:32
  57.0 11.5 %collective-permute-start.13 = (bf16[4,2,64,384]{3,2,1,0:T(8,128)(2,1)S(1)}, bf16[4,2,64,384]{3,2,1,0:T(8,128)(2,1)}, u32[]{:S(2)}, u32[]{:S(2)}) collective-permute-start(bf16[4,2,64,384]{3,2,1,0:T(8,128)(2,1)S(1)} %collective-permute-done.11.refs_10_), channel_id=1, source_target_pairs={{0,28},{1,29},{2,30},{3,31},{4,0},{5,1},{6,2},{7,3},{8,4},{9,5},{1... | collective-permute-start | bytes 1179656 | tf_op jit(solution)/shard_map/ppermute | solution.py:32
  60.7 17.0 %collective-permute-start.27 = (bf16[5,2,64,384]{3,2,1,0:T(8,128)(2,1)}, bf16[5,2,64,384]{3,2,1,0:T(8,128)(2,1)}, u32[]{:S(2)}, u32[]{:S(2)}) collective-permute-start(bf16[5,2,64,384]{3,2,1,0:T(8,128)(2,1)} %bitcast_dynamic-update-slice_fusion.refs_17_), channel_id=1, source_target_pairs={{0,96},{1,97},{2,98},{3,99},{4,100},{5,101},{6,102},{7,103},{8,104... | collective-permute-start | bytes 1474568 | tf_op jit(solution)/shard_map/ppermute | solution.py:32
  66.4 26.3 %collective-permute-start.2 = (bf16[128,4096]{1,0:T(8,128)(2,1)}, bf16[128,4096]{1,0:T(8,128)(2,1)S(1)}, u32[]{:S(2)}, u32[]{:S(2)}) collective-permute-start(bf16[128,4096]{1,0:T(8,128)(2,1)} %shard_map.120.refs_0_), channel_id=1, source_target_pairs={{0,2},{1,3},{2,0},{3,1},{4,6},{5,7},{6,4},{7,5},{8,10},{9,11},{10,... | collective-permute-start | bytes 3145736 | tf_op jit(solution)/shard_map/ppermute | solution.py:32
  68.1 41.6 %collective-permute-start.3 = (bf16[128,4096]{1,0:T(8,128)(2,1)S(1)}, bf16[128,4096]{1,0:T(8,128)(2,1)S(1)}, u32[]{:S(2)}, u32[]{:S(2)}) collective-permute-start(bf16[128,4096]{1,0:T(8,128)(2,1)S(1)} %copy-done.1), channel_id=1, source_target_pairs={{0,2},{1,3},{2,0},{3,1},{4,6},{5,7},{6,4},{7,5},{8,10},{9,11},{10,... | collective-permute-start | bytes 3145736 | tf_op jit(solution)/shard_map/ppermute | solution.py:32
  68.5 9.2 %collective-permute-start.12 = (bf16[4,2,64,384]{3,2,1,0:T(8,128)(2,1)}, bf16[4,2,64,384]{3,2,1,0:T(8,128)(2,1)S(1)}, u32[]{:S(2)}, u32[]{:S(2)}) collective-permute-start(bf16[4,2,64,384]{3,2,1,0:T(8,128)(2,1)} %collective-permute-done.10.refs_9_), channel_id=1, source_target_pairs={{0,4},{1,5},{2,6},{3,7},{4,8},{5,9},{6,10},{7,11},{8,12},{9,13},{1... | collective-permute-start | bytes 1179656 | tf_op jit(solution)/shard_map/ppermute | solution.py:32
  68.5 41.2 %collective-permute-start = (bf16[128,4096]{1,0:T(8,128)(2,1)}, bf16[128,4096]{1,0:T(8,128)(2,1)S(1)}, u32[]{:S(2)}, u32[]{:S(2)}) collective-permute-start(bf16[128,4096]{1,0:T(8,128)(2,1)} %shard_map.120.refs_0_), channel_id=1, source_target_pairs={{0,1},{1,0},{2,3},{3,2},{4,5},{5,4},{6,7},{7,6},{8,9},{9,8},{10,11... | collective-permute-start | bytes 3145736 | tf_op jit(solution)/shard_map/ppermute | solution.py:32
  77.7 32.1 %collective-permute-start.1 = (bf16[128,4096]{1,0:T(8,128)(2,1)S(1)}, bf16[128,4096]{1,0:T(8,128)(2,1)S(1)}, u32[]{:S(2)}, u32[]{:S(2)}) collective-permute-start(bf16[128,4096]{1,0:T(8,128)(2,1)S(1)} %copy-done.1), channel_id=1, source_target_pairs={{0,1},{1,0},{2,3},{3,2},{4,5},{5,4},{6,7},{7,6},{8,9},{9,8},{10,11... | collective-permute-start | bytes 3145736 | tf_op jit(solution)/shard_map/ppermute | solution.py:32
  77.7 14.9 %collective-permute-start.25 = (bf16[5,2,64,384]{3,2,1,0:T(8,128)(2,1)}, bf16[5,2,64,384]{3,2,1,0:T(8,128)(2,1)S(1)}, u32[]{:S(2)}, u32[]{:S(2)}) collective-permute-start(bf16[5,2,64,384]{3,2,1,0:T(8,128)(2,1)} %bitcast_dynamic-update-slice_fusion.refs_17_), channel_id=1, source_target_pairs={{0,32},{1,33},{2,34},{3,35},{4,36},{5,37},{6,38},{7,39},{8,40},{9,... | collective-permute-start | bytes 1474568 | tf_op jit(solution)/shard_map/ppermute | solution.py:32
  92.5 22.1 %collective-permute-start.32 = (bf16[2,320,512]{2,1,0:T(8,128)(2,1)}, bf16[2,320,512]{2,1,0:T(8,128)(2,1)S(1)}, u32[]{:S(2)}, u32[]{:S(2)}) collective-permute-start(bf16[2,320,512]{2,1,0:T(8,128)(2,1)} %collective-permute-done.31.refs_26_), channel_id=1, source_target_pairs={{0,1},{1,0},{2,3},{3,2},{4,5},{5,4},{6,7},{7,6},{8,9},{9,8},{10,11... | collective-permute-start | bytes 1966088 | tf_op jit(solution)/shard_map/ppermute | solution.py:32
  92.7 41.6 %collective-permute-start.4 = (bf16[128,4096]{1,0:T(8,128)(2,1)S(1)}, bf16[128,4096]{1,0:T(8,128)(2,1)S(1)}, u32[]{:S(2)}, u32[]{:S(2)}) collective-permute-start(bf16[128,4096]{1,0:T(8,128)(2,1)S(1)} %collective-permute-done.2.refs_4_), channel_id=1, source_target_pairs={{0,1},{1,0},{2,3},{3,2},{4,5},{5,4},{6,7},{7,6},{8,9},{9,8},{10,11... | collective-permute-start | bytes 3145736 | tf_op jit(solution)/shard_map/ppermute | solution.py:32
  109.7 24.6 %collective-permute-start.5 = (bf16[128,4096]{1,0:T(8,128)(2,1)S(1)}, bf16[128,4096]{1,0:T(8,128)(2,1)S(1)}, u32[]{:S(2)}, u32[]{:S(2)}) collective-permute-start(bf16[128,4096]{1,0:T(8,128)(2,1)S(1)} %collective-permute-done.3.refs_5_), channel_id=1, source_target_pairs={{0,1},{1,0},{2,3},{3,2},{4,5},{5,4},{6,7},{7,6},{8,9},{9,8},{10,11... | collective-permute-start | bytes 3145736 | tf_op jit(solution)/shard_map/ppermute | solution.py:32
  109.7 12.7 %collective-permute-start.14 = (bf16[4,2,64,384]{3,2,1,0:T(8,128)(2,1)S(1)}, bf16[4,2,64,384]{3,2,1,0:T(8,128)(2,1)S(1)}, u32[]{:S(2)}, u32[]{:S(2)}) collective-permute-start(bf16[4,2,64,384]{3,2,1,0:T(8,128)(2,1)S(1)} %collective-permute-done.12.refs_11_), channel_id=1, source_target_pairs={{0,4},{1,5},{2,6},{3,7},{4,8},{5,9},{6,10},{7,11},{8,12},{9,13},{1... | collective-permute-start | bytes 1179656 | tf_op jit(solution)/shard_map/ppermute | solution.py:32
  111.7 14.4 %collective-permute-start.29 = (bf16[5,2,64,384]{3,2,1,0:T(8,128)(2,1)}, bf16[5,2,64,384]{3,2,1,0:T(8,128)(2,1)S(1)}, u32[]{:S(2)}, u32[]{:S(2)}) collective-permute-start(bf16[5,2,64,384]{3,2,1,0:T(8,128)(2,1)} %collective-permute-done.27.refs_21_), channel_id=1, source_target_pairs={{0,96},{1,97},{2,98},{3,99},{4,100},{5,101},{6,102},{7,103},{8,104... | collective-permute-start | bytes 1474568 | tf_op jit(solution)/shard_map/ppermute | solution.py:32
  114.6 11.5 %collective-permute-start.15 = (bf16[4,2,64,384]{3,2,1,0:T(8,128)(2,1)}, bf16[4,2,64,384]{3,2,1,0:T(8,128)(2,1)S(1)}, u32[]{:S(2)}, u32[]{:S(2)}) collective-permute-start(bf16[4,2,64,384]{3,2,1,0:T(8,128)(2,1)} %collective-permute-done.13.refs_12_), channel_id=1, source_target_pairs={{0,28},{1,29},{2,30},{3,31},{4,0},{5,1},{6,2},{7,3},{8,4},{9,5},{1... | collective-permute-start | bytes 1179656 | tf_op jit(solution)/shard_map/ppermute | solution.py:32
  122.4 11.8 %collective-permute-start.16 = (bf16[4,2,64,384]{3,2,1,0:T(8,128)(2,1)S(1)}, bf16[4,2,64,384]{3,2,1,0:T(8,128)(2,1)S(1)}, u32[]{:S(2)}, u32[]{:S(2)}) collective-permute-start(bf16[4,2,64,384]{3,2,1,0:T(8,128)(2,1)S(1)} %collective-permute-done.14.refs_13_), channel_id=1, source_target_pairs={{0,4},{1,5},{2,6},{3,7},{4,8},{5,9},{6,10},{7,11},{8,12},{9,13},{1... | collective-permute-start | bytes 1179656 | tf_op jit(solution)/shard_map/ppermute | solution.py:32
  163.2 28.0 %all-to-all-start = ((bf16[256,2,256]{2,1,0:T(2,128)(2,1)}), bf16[256,2,256]{2,1,0:T(2,128)(2,1)S(1)}, u32[]{:S(2)}, u32[]{:S(2)}) async-start(bf16[256,2,256]{2,1,0:T(2,128)(2,1)} %reshape.40), calls=%async_computation | async-start | bytes 524288 | tf_op jit(solution)/shard_map/all_to_all | solution.py:471
  176.4 22.0 %collective-permute-start.34 = (bf16[2,256,512]{2,1,0:T(8,128)(2,1)}, bf16[2,256,512]{2,1,0:T(8,128)(2,1)S(1)}, u32[]{:S(2)}, u32[]{:S(2)}) collective-permute-start(bf16[2,256,512]{2,1,0:T(8,128)(2,1)} %get-tuple-element.22), channel_id=1, source_target_pairs={{0,2},{1,3},{2,0},{3,1},{4,6},{5,7},{6,4},{7,5},{8,10},{9,11},{10,... | collective-permute-start | bytes 1572872 | tf_op jit(solution)/shard_map/ppermute | solution.py:32
  192.5 19.1 %all-to-all-start.1 = ((bf16[64,2,1024]{2,1,0:T(2,128)(2,1)}), bf16[64,2,1024]{2,1,0:T(2,128)(2,1)S(1)}, u32[]{:S(2)}, u32[]{:S(2)}) async-start(bf16[64,2,1024]{2,1,0:T(2,128)(2,1)} %broadcast_in_dim.2), calls=%async_computation.1 | async-start | bytes 524288 | tf_op jit(solution)/shard_map/all_to_all | solution.py:57
  198.4 14.7 %collective-permute-start.35 = (bf16[2,256,512]{2,1,0:T(8,128)(2,1)S(1)}, bf16[2,256,512]{2,1,0:T(8,128)(2,1)S(1)}, u32[]{:S(2)}, u32[]{:S(2)}) collective-permute-start(bf16[2,256,512]{2,1,0:T(8,128)(2,1)S(1)} %collective-permute-done.34.refs_2_), channel_id=1, source_target_pairs={{0,1},{1,0},{2,3},{3,2},{4,5},{5,4},{6,7},{7,6},{8,9},{9,8},{10,11... | collective-permute-start | bytes 1572872 | tf_op jit(solution)/shard_map/ppermute | solution.py:32
  198.5 14.6 %collective-permute-start.33 = (bf16[256,512]{1,0:T(8,128)(2,1)}, bf16[256,512]{1,0:T(8,128)(2,1)}, u32[]{:S(2)}, u32[]{:S(2)}) collective-permute-start(bf16[256,512]{1,0:T(8,128)(2,1)} %get-tuple-element.21), channel_id=1, source_target_pairs={{0,1},{1,0},{2,3},{3,2},{4,5},{5,4},{6,7},{7,6},{8,9},{9,8},{10,11... | collective-permute-start | bytes 786440 | tf_op jit(solution)/shard_map/ppermute | solution.py:32
  (30 other events, 504.6 us)

commit v2 on v1

--- a/solution.py
+++ b/solution.py
@@ -319,20 +319,17 @@
         return dot(queries[head], dscore, 0, 0)
 
     score_out, soft_out, attend_out = {}, {}, {}
-    for tick in range(GROUP + 3):
+    for tick in range(GROUP + 4):
         if tick < GROUP:
             score_out[tick] = scores(tick)
         if 0 <= tick - 2 < GROUP:
             attend_out[tick - 2] = attend(tick - 2, soft_out[tick - 2])
-            value_sum += attend_out[tick - 2][2]
+            sums[HEAD_SIZE:, :] += attend_out[tick - 2][2]
         if 0 <= tick - 1 < GROUP:
             soft_out[tick - 1] = soft(score_out[tick - 1])
-        if 0 <= tick - 3 < GROUP:
-            attended, dprob, _ = attend_out[tick - 3]
-            key_sum += back(tick - 3, soft_out[tick - 3][0], attended, dprob)
-    sums[0:HEAD_SIZE, :] += key_sum * HEAD_SIZE ** (-0.5)
-    sums[HEAD_SIZE:, :] += value_sum
-
+        if 0 <= tick - 4 < GROUP:
+            attended, dprob, _ = attend_out[tick - 4]
+            sums[0:HEAD_SIZE, :] += back(tick - 4, soft_out[tick - 4][0], attended, dprob) * HEAD_SIZE ** (-0.5)
     for index in range(4):
 
         @pl.when(step == index)
@@ -405,7 +402,7 @@
     for _ in range(3):
         ups.append(permute(ups[-1], along_z(1)))
         downs.append(permute(downs[-1], along_z(-1)))
-    last = permute(ups[3], along_z(1))
+    last = permute(downs[3], along_z(-1))
     near = jnp.stack([second, ups[1], downs[1]])
     rest = jnp.stack([ups[2], downs[2], ups[3], downs[3], last])
     near_up, near_down = permute(near, along_x(1)), permute(near, along_x(-1))

time: 219 us -> 214 us (0.977)
  waiting for transfers between devices: 99 us -> 94.5 us
    ppermute x36, waiting for transfers between devices: 73.1 us -> 68.6 us  [permute(): return lax.ppermute(value, MESH_AXES, pairs)]
where the time goes in v2:
time: 214 us; the launch traced here: 212 us
  waiting for transfers between devices  94.5 us (44%)
  starting transfers between devices  62.7 us (29%)
  Pallas kernels  36.4 us (17%)
  local copies, waits for them, and re-layouts  14 us (7%)
  other arithmetic  3.14 us (1%)
    ppermute x36, waiting for transfers between devices, permute(): return lax.ppermute(value, MESH_AXES, pairs)  68.6 us
    ppermute x36, starting transfers between devices, permute(): return lax.ppermute(value, MESH_AXES, pairs)  44.4 us
    pallas_call x1, Pallas kernels, layer(): pl.pallas_call(layer_kernel, grid_spec=pltpu.PrefetchScalarGridSpec(num_s...  24 us
    all_to_all x1, waiting for transfers between devices, layer_step(): lax.all_to_all(gradient.reshape(256, 2, 256), ('owner', 'fsdp', 'dp'), 0,...  13.3 us
    all_to_all x1, waiting for transfers between devices, spread(): return lax.all_to_all(copies, axes, 0, 0, tiled=True)  12.6 us
    all_to_all x1, starting transfers between devices, layer_step(): lax.all_to_all(gradient.reshape(256, 2, 256), ('owner', 'fsdp', 'dp'), 0,...  12.4 us
    unnamed x52, local copies, waits for them, and re-layouts  8.11 us
    all_to_all x1, starting transfers between devices, spread(): return lax.all_to_all(copies, axes, 0, 0, tiled=True)  5.86 us
  transfers between devices with their start and end apart: 38, of which 17 were waited for; matrix products, arithmetic and copies ran while one was open for 4% of the time, Pallas kernels for 4%

profile of v2, /device:TPU:2, one launch (start us, length us, event | category | flops | bytes accessed | tf_op | source)
XLA Modules:
  0.0 212.4 jit_solution(13719894482500086182)
XLA Ops:
  2.4 3.1 %collective-permute-start.6 = (bf16[64,768]{1,0:T(8,128)(2,1)S(1)}, bf16[64,768]{1,0:T(8,128)(2,1)S(1)}, u32[]{:S(2)}, u32[]{:S(2)}) collective-permute-start(bf16[64,768]{1,0:T(8,128)(2,1)S(1)} %get-tuple-element.16), channel_id=1, source_target_pairs={{0,130},{1,131},{2,128},{3,129},{4,134},{5,135},{6,132},{7,133},{8... | collective-permute-start | bytes 294920 | tf_op jit(solution)/shard_map/ppermute | solution.py:32
  5.5 2.8 %collective-permute-done.6 = bf16[64,768]{1,0:T(8,128)(2,1)S(1)} collective-permute-done((bf16[64,768]{1,0:T(8,128)(2,1)S(1)}, bf16[64,768]{1,0:T(8,128)(2,1)S(1)}, u32[]{:S(2)}, u32[]{:S(2)}) %collective-permute-start.6) | collective-permute-done | bytes 98336 | tf_op jit(solution)/shard_map/ppermute | solution.py:32
  8.3 2.0 collective-permute-start.17
  10.3 4.0 %collective-permute-start.18 = (bf16[2,64,384]{2,1,0:T(8,128)(2,1)S(1)}, bf16[2,64,384]{2,1,0:T(8,128)(2,1)S(1)}, u32[]{:S(2)}, u32[]{:S(2)}) collective-permute-start(bf16[2,64,384]{2,1,0:T(8,128)(2,1)S(1)} %get-tuple-element.29), channel_id=1, source_target_pairs={{0,28},{1,29},{2,30},{3,31},{4,0},{5,1},{6,2},{7,3},{8,4},{9,5},{1... | collective-permute-start | bytes 294920 | tf_op jit(solution)/shard_map/ppermute | solution.py:32
  15.6 4.0 %shard_map.122 = (bf16[320,512]{1,0:T(8,128)(2,1)}, bf16[320,512]{1,0:T(8,128)(2,1)}, bf16[2,320,512]{2,1,0:T(8,128)(2,1)}) custom-call(s32[5]{0:T(128)} %stack.73.place, bf16[1,256,2048]{2,1,0:T(8,128)(2,1)} %cotangent.1, f32[128,1024]{1,0:T(8,128)} %value_rows.1, f32[128,1024]{1,0:T(8,128)} %value_rows.1), custom_call_target="tpu_custom_call" | custom-call | tf_op jit(solution)/shard_map/pallas_call | solution.py:119
  20.5 2.4 %collective-permute-start.8 = (bf16[2,64,384]{2,1,0:T(8,128)(2,1)S(1)}, bf16[2,64,384]{2,1,0:T(8,128)(2,1)S(1)}, u32[]{:S(2)}, u32[]{:S(2)}) collective-permute-start(bf16[2,64,384]{2,1,0:T(8,128)(2,1)S(1)} %get-tuple-element.30), channel_id=1, source_target_pairs={{0,64},{1,65},{2,66},{3,67},{4,68},{5,69},{6,70},{7,71},{8,72},{9,... | collective-permute-start | bytes 294920 | tf_op jit(solution)/shard_map/ppermute | solution.py:32
  22.9 1.8 collective-permute-start.7
  24.9 2.2 %collective-permute-start.24 = (bf16[3,2,64,384]{3,2,1,0:T(8,128)(2,1)S(1)}, bf16[3,2,64,384]{3,2,1,0:T(8,128)(2,1)}, u32[]{:S(2)}, u32[]{:S(2)}) collective-permute-start(bf16[3,2,64,384]{3,2,1,0:T(8,128)(2,1)S(1)} %pad_maximum_fusion.1.refs_16_), channel_id=1, source_target_pairs={{0,32},{1,33},{2,34},{3,35},{4,36},{5,37},{6,38},{7,39},{8,40},{9,... | collective-permute-start | bytes 884744 | tf_op jit(solution)/shard_map/ppermute | solution.py:32
  29.7 1.9 collective-permute-start.20
  31.7 2.1 collective-permute-done.19
  34.4 3.2 %collective-permute-start.22 = (bf16[2,64,384]{2,1,0:T(8,128)(2,1)S(1)}, bf16[2,64,384]{2,1,0:T(8,128)(2,1)S(1)}, u32[]{:S(2)}, u32[]{:S(2)}) collective-permute-start(bf16[2,64,384]{2,1,0:T(8,128)(2,1)S(1)} %collective-permute-done.20), channel_id=1, source_target_pairs={{0,28},{1,29},{2,30},{3,31},{4,0},{5,1},{6,2},{7,3},{8,4},{9,5},{1... | collective-permute-start | bytes 294920 | tf_op jit(solution)/shard_map/ppermute | solution.py:32
  40.8 3.7 %collective-permute-start.23 = (bf16[2,64,384]{2,1,0:T(8,128)(2,1)S(1)}, bf16[2,64,384]{2,1,0:T(8,128)(2,1)S(1)}, u32[]{:S(2)}, u32[]{:S(2)}) collective-permute-start(bf16[2,64,384]{2,1,0:T(8,128)(2,1)S(1)} %collective-permute-done.22), channel_id=1, source_target_pairs={{0,28},{1,29},{2,30},{3,31},{4,0},{5,1},{6,2},{7,3},{8,4},{9,5},{1... | collective-permute-start | bytes 294920 | tf_op jit(solution)/shard_map/ppermute | solution.py:32
  45.2 2.5 %collective-permute-start.26 = (bf16[3,2,64,384]{3,2,1,0:T(8,128)(2,1)S(1)}, bf16[3,2,64,384]{3,2,1,0:T(8,128)(2,1)S(1)}, u32[]{:S(2)}, u32[]{:S(2)}) collective-permute-start(bf16[3,2,64,384]{3,2,1,0:T(8,128)(2,1)S(1)} %pad_maximum_fusion.1.refs_16_), channel_id=1, source_target_pairs={{0,96},{1,97},{2,98},{3,99},{4,100},{5,101},{6,102},{7,103},{8,104... | collective-permute-start | bytes 884744 | tf_op jit(solution)/shard_map/ppermute | solution.py:32
  47.7 2.1 collective-permute-done.23
  50.6 2.7 %collective-permute-start.28 = (bf16[3,2,64,384]{3,2,1,0:T(8,128)(2,1)}, bf16[3,2,64,384]{3,2,1,0:T(8,128)(2,1)}, u32[]{:S(2)}, u32[]{:S(2)}) collective-permute-start(bf16[3,2,64,384]{3,2,1,0:T(8,128)(2,1)} %collective-permute-done.24.refs_18_), channel_id=1, source_target_pairs={{0,32},{1,33},{2,34},{3,35},{4,36},{5,37},{6,38},{7,39},{8,40},{9,... | collective-permute-start | bytes 884744 | tf_op jit(solution)/shard_map/ppermute | solution.py:32
  53.3 3.2 %collective-permute-start.13 = (bf16[4,2,64,384]{3,2,1,0:T(8,128)(2,1)S(1)}, bf16[4,2,64,384]{3,2,1,0:T(8,128)(2,1)}, u32[]{:S(2)}, u32[]{:S(2)}) collective-permute-start(bf16[4,2,64,384]{3,2,1,0:T(8,128)(2,1)S(1)} %collective-permute-done.11.refs_10_), channel_id=1, source_target_pairs={{0,28},{1,29},{2,30},{3,31},{4,0},{5,1},{6,2},{7,3},{8,4},{9,5},{1... | collective-permute-start | bytes 1179656 | tf_op jit(solution)/shard_map/ppermute | solution.py:32
  57.8 2.4 %shard_map.121.refs_1_ = bf16[128,4096]{1,0:T(8,128)(2,1)} custom-call(bf16[1,256,4096]{2,1,0:T(8,128)(2,1)} %states.1, f32[1,4096]{1,0:T(1,128)} %bitcast.34), custom_call_target="tpu_custom_call" | custom-call | tf_op jit(solution)/shard_map/pallas_call | solution.py:85
  60.3 2.5 %shard_map.120.refs_0_ = bf16[128,4096]{1,0:T(8,128)(2,1)} custom-call(bf16[1,256,4096]{2,1,0:T(8,128)(2,1)} %states.1, f32[1,4096]{1,0:T(1,128)} %bitcast.35), custom_call_target="tpu_custom_call" | custom-call | tf_op jit(solution)/shard_map/pallas_call | solution.py:85
  65.0 9.1 %collective-permute-done.12.refs_11_ = bf16[4,2,64,384]{3,2,1,0:T(8,128)(2,1)S(1)} collective-permute-done((bf16[4,2,64,384]{3,2,1,0:T(8,128)(2,1)}, bf16[4,2,64,384]{3,2,1,0:T(8,128)(2,1)S(1)}, u32[]{:S(2)}, u32[]{:S(2)}) %collective-permute-start.12) | collective-permute-done | bytes 393248 | tf_op jit(solution)/shard_map/ppermute | solution.py:32
  75.5 12.8 %collective-permute-done.25.refs_19_ = bf16[5,2,64,384]{3,2,1,0:T(8,128)(2,1)S(1)} collective-permute-done((bf16[5,2,64,384]{3,2,1,0:T(8,128)(2,1)}, bf16[5,2,64,384]{3,2,1,0:T(8,128)(2,1)S(1)}, u32[]{:S(2)}, u32[]{:S(2)}) %collective-permute-start.25) | collective-permute-done | bytes 491552 | tf_op jit(solution)/shard_map/ppermute | solution.py:32
  89.1 17.4 %collective-permute-done.3.refs_5_ = bf16[128,4096]{1,0:T(8,128)(2,1)S(1)} collective-permute-done((bf16[128,4096]{1,0:T(8,128)(2,1)S(1)}, bf16[128,4096]{1,0:T(8,128)(2,1)S(1)}, u32[]{:S(2)}, u32[]{:S(2)}) %collective-permute-start.3) | collective-permute-done | bytes 1048608 | tf_op jit(solution)/shard_map/ppermute | solution.py:32
  108.5 2.4 %collective-permute-start.29 = (bf16[5,2,64,384]{3,2,1,0:T(8,128)(2,1)}, bf16[5,2,64,384]{3,2,1,0:T(8,128)(2,1)S(1)}, u32[]{:S(2)}, u32[]{:S(2)}) collective-permute-start(bf16[5,2,64,384]{3,2,1,0:T(8,128)(2,1)} %collective-permute-done.27.refs_21_), channel_id=1, source_target_pairs={{0,96},{1,97},{2,98},{3,99},{4,100},{5,101},{6,102},{7,103},{8,104... | collective-permute-start | bytes 1474568 | tf_op jit(solution)/shard_map/ppermute | solution.py:32
  110.9 2.4 %collective-permute-start.15 = (bf16[4,2,64,384]{3,2,1,0:T(8,128)(2,1)}, bf16[4,2,64,384]{3,2,1,0:T(8,128)(2,1)S(1)}, u32[]{:S(2)}, u32[]{:S(2)}) collective-permute-start(bf16[4,2,64,384]{3,2,1,0:T(8,128)(2,1)} %collective-permute-done.13.refs_12_), channel_id=1, source_target_pairs={{0,28},{1,29},{2,30},{3,31},{4,0},{5,1},{6,2},{7,3},{8,4},{9,5},{1... | collective-permute-start | bytes 1179656 | tf_op jit(solution)/shard_map/ppermute | solution.py:32
  113.2 6.0 %collective-permute-done.14.refs_13_ = bf16[4,2,64,384]{3,2,1,0:T(8,128)(2,1)S(1)} collective-permute-done((bf16[4,2,64,384]{3,2,1,0:T(8,128)(2,1)S(1)}, bf16[4,2,64,384]{3,2,1,0:T(8,128)(2,1)S(1)}, u32[]{:S(2)}, u32[]{:S(2)}) %collective-permute-start.14) | collective-permute-done | bytes 393248 | tf_op jit(solution)/shard_map/ppermute | solution.py:32
  122.4 8.6 %collective-permute-done.16.refs_15_ = bf16[4,2,64,384]{3,2,1,0:T(8,128)(2,1)S(1)} collective-permute-done((bf16[4,2,64,384]{3,2,1,0:T(8,128)(2,1)S(1)}, bf16[4,2,64,384]{3,2,1,0:T(8,128)(2,1)S(1)}, u32[]{:S(2)}, u32[]{:S(2)}) %collective-permute-start.16) | collective-permute-done | bytes 393248 | tf_op jit(solution)/shard_map/ppermute | solution.py:32
  133.1 24.0 %shard_map.123 = (bf16[256,512]{1,0:T(8,128)(2,1)}, bf16[256,512]{1,0:T(8,128)(2,1)}, bf16[2,256,512]{2,1,0:T(8,128)(2,1)}, bf16[512,256]{1,0:T(8,128)(2,1)}) custom-call(s32[5]{0:T(128)} %stack.73.place, bf16[128,4096]{1,0:T(8,128)(2,1)} %shard_map.120.refs_0_, bf16[128,4096]{1,0:T(8,128)(2,1)} %shard_map.121.refs_1_, bf16[128,4096]{1,0:T(8,128)(2,1)} %copy-done.6, ...), custom_call_target="tpu_custom_call" | custom-call | tf_op jit(solution)/shard_map/pallas_call | solution.py:353
  157.2 1.9 reshape.40
  159.0 12.4 %all-to-all-start = ((bf16[256,2,256]{2,1,0:T(2,128)(2,1)}), bf16[256,2,256]{2,1,0:T(2,128)(2,1)S(1)}, u32[]{:S(2)}, u32[]{:S(2)}) async-start(bf16[256,2,256]{2,1,0:T(2,128)(2,1)} %reshape.40), calls=%async_computation | async-start | bytes 524288 | tf_op jit(solution)/shard_map/all_to_all | solution.py:468
  173.0 13.3 %all-to-all-done = bf16[256,2,256]{2,1,0:T(2,128)(2,1)S(1)} async-done(((bf16[256,2,256]{2,1,0:T(2,128)(2,1)}), bf16[256,2,256]{2,1,0:T(2,128)(2,1)S(1)}, u32[]{:S(2)}, u32[]{:S(2)}) %all-to-all-start) | async-done | bytes 262176 | tf_op jit(solution)/shard_map/all_to_all | solution.py:468
  187.5 5.9 %all-to-all-start.1 = ((bf16[64,2,1024]{2,1,0:T(2,128)(2,1)}), bf16[64,2,1024]{2,1,0:T(2,128)(2,1)S(1)}, u32[]{:S(2)}, u32[]{:S(2)}) async-start(bf16[64,2,1024]{2,1,0:T(2,128)(2,1)} %broadcast_in_dim.2), calls=%async_computation.1 | async-start | bytes 524288 | tf_op jit(solution)/shard_map/all_to_all | solution.py:57
  194.0 12.6 %all-to-all-done.1 = bf16[64,2,1024]{2,1,0:T(2,128)(2,1)S(1)} async-done(((bf16[64,2,1024]{2,1,0:T(2,128)(2,1)}), bf16[64,2,1024]{2,1,0:T(2,128)(2,1)S(1)}, u32[]{:S(2)}, u32[]{:S(2)}) %all-to-all-start.1) | async-done | bytes 262176 | tf_op jit(solution)/shard_map/all_to_all | solution.py:57
  208.9 3.5 %shard_map.124 = bf16[1,256,2048]{2,1,0:T(8,128)(2,1)} custom-call(s32[5]{0:T(128)} %stack.73.place, bf16[256,512]{1,0:T(8,128)(2,1)} %get-tuple-element.20.refs_0_, bf16[256,512]{1,0:T(8,128)(2,1)} %collective-permute-done.33.refs_1_, bf16[2,256,512]{2,1,0:T(8,128)(2,1)} %copy-done.13, bf16[2,256,512]{2,1,0:T(8,128)(2,1)} %copy-done.14), custom_call_target="tpu_custom_call" | custom-call | tf_op jit(solution)/shard_map/pallas_call | solution.py:147
  (121 shorter events, 30.0 us)
Async XLA Ops:
  8.3 12.2 %collective-permute-start.17 = (bf16[2,64,384]{2,1,0:T(8,128)(2,1)S(1)}, bf16[2,64,384]{2,1,0:T(8,128)(2,1)S(1)}, u32[]{:S(2)}, u32[]{:S(2)}) collective-permute-start(bf16[2,64,384]{2,1,0:T(8,128)(2,1)S(1)} %get-tuple-element.29), channel_id=1, source_target_pairs={{0,4},{1,5},{2,6},{3,7},{4,8},{5,9},{6,10},{7,11},{8,12},{9,13},{1... | collective-permute-start | bytes 294920 | tf_op jit(solution)/shard_map/ppermute | solution.py:32
  10.3 12.7 %collective-permute-start.18 = (bf16[2,64,384]{2,1,0:T(8,128)(2,1)S(1)}, bf16[2,64,384]{2,1,0:T(8,128)(2,1)S(1)}, u32[]{:S(2)}, u32[]{:S(2)}) collective-permute-start(bf16[2,64,384]{2,1,0:T(8,128)(2,1)S(1)} %get-tuple-element.29), channel_id=1, source_target_pairs={{0,28},{1,29},{2,30},{3,31},{4,0},{5,1},{6,2},{7,3},{8,4},{9,5},{1... | collective-permute-start | bytes 294920 | tf_op jit(solution)/shard_map/ppermute | solution.py:32
  19.6 25.6 %collective-permute-start.30 = (bf16[320,512]{1,0:T(8,128)(2,1)}, bf16[320,512]{1,0:T(8,128)(2,1)S(1)}, u32[]{:S(2)}, u32[]{:S(2)}) collective-permute-start(bf16[320,512]{1,0:T(8,128)(2,1)} %get-tuple-element.18), channel_id=1, source_target_pairs={{0,1},{1,0},{2,3},{3,2},{4,5},{5,4},{6,7},{7,6},{8,9},{9,8},{10,11... | collective-permute-start | bytes 983048 | tf_op jit(solution)/shard_map/ppermute | solution.py:32
  19.6 44.9 %collective-permute-start.31 = (bf16[2,320,512]{2,1,0:T(8,128)(2,1)}, bf16[2,320,512]{2,1,0:T(8,128)(2,1)}, u32[]{:S(2)}, u32[]{:S(2)}) collective-permute-start(bf16[2,320,512]{2,1,0:T(8,128)(2,1)} %get-tuple-element.19), channel_id=1, source_target_pairs={{0,2},{1,3},{2,0},{3,1},{4,6},{5,7},{6,4},{7,5},{8,10},{9,11},{10,... | collective-permute-start | bytes 1966088 | tf_op jit(solution)/shard_map/ppermute | solution.py:32
  20.5 7.4 %collective-permute-start.8 = (bf16[2,64,384]{2,1,0:T(8,128)(2,1)S(1)}, bf16[2,64,384]{2,1,0:T(8,128)(2,1)S(1)}, u32[]{:S(2)}, u32[]{:S(2)}) collective-permute-start(bf16[2,64,384]{2,1,0:T(8,128)(2,1)S(1)} %get-tuple-element.30), channel_id=1, source_target_pairs={{0,64},{1,65},{2,66},{3,67},{4,68},{5,69},{6,70},{7,71},{8,72},{9,... | collective-permute-start | bytes 294920 | tf_op jit(solution)/shard_map/ppermute | solution.py:32
  22.9 6.8 %collective-permute-start.7 = (bf16[2,64,384]{2,1,0:T(8,128)(2,1)S(1)}, bf16[2,64,384]{2,1,0:T(8,128)(2,1)S(1)}, u32[]{:S(2)}, u32[]{:S(2)}) collective-permute-start(bf16[2,64,384]{2,1,0:T(8,128)(2,1)S(1)} %get-tuple-element.30), channel_id=1, source_target_pairs={{0,32},{1,33},{2,34},{3,35},{4,36},{5,37},{6,38},{7,39},{8,40},{9,... | collective-permute-start | bytes 294920 | tf_op jit(solution)/shard_map/ppermute | solution.py:32
  24.9 25.7 %collective-permute-start.24 = (bf16[3,2,64,384]{3,2,1,0:T(8,128)(2,1)S(1)}, bf16[3,2,64,384]{3,2,1,0:T(8,128)(2,1)}, u32[]{:S(2)}, u32[]{:S(2)}) collective-permute-start(bf16[3,2,64,384]{3,2,1,0:T(8,128)(2,1)S(1)} %pad_maximum_fusion.1.refs_16_), channel_id=1, source_target_pairs={{0,32},{1,33},{2,34},{3,35},{4,36},{5,37},{6,38},{7,39},{8,40},{9,... | collective-permute-start | bytes 884744 | tf_op jit(solution)/shard_map/ppermute | solution.py:32
  39.6 13.7 %collective-permute-start.11 = (bf16[4,2,64,384]{3,2,1,0:T(8,128)(2,1)S(1)}, bf16[4,2,64,384]{3,2,1,0:T(8,128)(2,1)S(1)}, u32[]{:S(2)}, u32[]{:S(2)}) collective-permute-start(bf16[4,2,64,384]{3,2,1,0:T(8,128)(2,1)S(1)} %pad_maximum_fusion.refs_8_), channel_id=1, source_target_pairs={{0,28},{1,29},{2,30},{3,31},{4,0},{5,1},{6,2},{7,3},{8,4},{9,5},{1... | collective-permute-start | bytes 1179656 | tf_op jit(solution)/shard_map/ppermute | solution.py:32
  40.8 8.9 %collective-permute-start.23 = (bf16[2,64,384]{2,1,0:T(8,128)(2,1)S(1)}, bf16[2,64,384]{2,1,0:T(8,128)(2,1)S(1)}, u32[]{:S(2)}, u32[]{:S(2)}) collective-permute-start(bf16[2,64,384]{2,1,0:T(8,128)(2,1)S(1)} %collective-permute-done.22), channel_id=1, source_target_pairs={{0,28},{1,29},{2,30},{3,31},{4,0},{5,1},{6,2},{7,3},{8,4},{9,5},{1... | collective-permute-start | bytes 294920 | tf_op jit(solution)/shard_map/ppermute | solution.py:32
  45.2 11.9 %collective-permute-start.26 = (bf16[3,2,64,384]{3,2,1,0:T(8,128)(2,1)S(1)}, bf16[3,2,64,384]{3,2,1,0:T(8,128)(2,1)S(1)}, u32[]{:S(2)}, u32[]{:S(2)}) collective-permute-start(bf16[3,2,64,384]{3,2,1,0:T(8,128)(2,1)S(1)} %pad_maximum_fusion.1.refs_16_), channel_id=1, source_target_pairs={{0,96},{1,97},{2,98},{3,99},{4,100},{5,101},{6,102},{7,103},{8,104... | collective-permute-start | bytes 884744 | tf_op jit(solution)/shard_map/ppermute | solution.py:32
  49.8 13.0 %collective-permute-start.10 = (bf16[4,2,64,384]{3,2,1,0:T(8,128)(2,1)S(1)}, bf16[4,2,64,384]{3,2,1,0:T(8,128)(2,1)}, u32[]{:S(2)}, u32[]{:S(2)}) collective-permute-start(bf16[4,2,64,384]{3,2,1,0:T(8,128)(2,1)S(1)} %pad_maximum_fusion.refs_8_), channel_id=1, source_target_pairs={{0,4},{1,5},{2,6},{3,7},{4,8},{5,9},{6,10},{7,11},{8,12},{9,13},{1... | collective-permute-start | bytes 1179656 | tf_op jit(solution)/shard_map/ppermute | solution.py:32
  50.6 14.3 %collective-permute-start.28 = (bf16[3,2,64,384]{3,2,1,0:T(8,128)(2,1)}, bf16[3,2,64,384]{3,2,1,0:T(8,128)(2,1)}, u32[]{:S(2)}, u32[]{:S(2)}) collective-permute-start(bf16[3,2,64,384]{3,2,1,0:T(8,128)(2,1)} %collective-permute-done.24.refs_18_), channel_id=1, source_target_pairs={{0,32},{1,33},{2,34},{3,35},{4,36},{5,37},{6,38},{7,39},{8,40},{9,... | collective-permute-start | bytes 884744 | tf_op jit(solution)/shard_map/ppermute | solution.py:32
  53.3 11.6 %collective-permute-start.13 = (bf16[4,2,64,384]{3,2,1,0:T(8,128)(2,1)S(1)}, bf16[4,2,64,384]{3,2,1,0:T(8,128)(2,1)}, u32[]{:S(2)}, u32[]{:S(2)}) collective-permute-start(bf16[4,2,64,384]{3,2,1,0:T(8,128)(2,1)S(1)} %collective-permute-done.11.refs_10_), channel_id=1, source_target_pairs={{0,28},{1,29},{2,30},{3,31},{4,0},{5,1},{6,2},{7,3},{8,4},{9,5},{1... | collective-permute-start | bytes 1179656 | tf_op jit(solution)/shard_map/ppermute | solution.py:32
  57.1 17.0 %collective-permute-start.27 = (bf16[5,2,64,384]{3,2,1,0:T(8,128)(2,1)}, bf16[5,2,64,384]{3,2,1,0:T(8,128)(2,1)}, u32[]{:S(2)}, u32[]{:S(2)}) collective-permute-start(bf16[5,2,64,384]{3,2,1,0:T(8,128)(2,1)} %bitcast_dynamic-update-slice_fusion.refs_17_), channel_id=1, source_target_pairs={{0,96},{1,97},{2,98},{3,99},{4,100},{5,101},{6,102},{7,103},{8,104... | collective-permute-start | bytes 1474568 | tf_op jit(solution)/shard_map/ppermute | solution.py:32
  62.8 26.3 %collective-permute-start.2 = (bf16[128,4096]{1,0:T(8,128)(2,1)}, bf16[128,4096]{1,0:T(8,128)(2,1)S(1)}, u32[]{:S(2)}, u32[]{:S(2)}) collective-permute-start(bf16[128,4096]{1,0:T(8,128)(2,1)} %shard_map.120.refs_0_), channel_id=1, source_target_pairs={{0,2},{1,3},{2,0},{3,1},{4,6},{5,7},{6,4},{7,5},{8,10},{9,11},{10,... | collective-permute-start | bytes 3145736 | tf_op jit(solution)/shard_map/ppermute | solution.py:32
  64.5 41.9 %collective-permute-start.3 = (bf16[128,4096]{1,0:T(8,128)(2,1)S(1)}, bf16[128,4096]{1,0:T(8,128)(2,1)S(1)}, u32[]{:S(2)}, u32[]{:S(2)}) collective-permute-start(bf16[128,4096]{1,0:T(8,128)(2,1)S(1)} %copy-done.1), channel_id=1, source_target_pairs={{0,2},{1,3},{2,0},{3,1},{4,6},{5,7},{6,4},{7,5},{8,10},{9,11},{10,... | collective-permute-start | bytes 3145736 | tf_op jit(solution)/shard_map/ppermute | solution.py:32
  64.9 9.2 %collective-permute-start.12 = (bf16[4,2,64,384]{3,2,1,0:T(8,128)(2,1)}, bf16[4,2,64,384]{3,2,1,0:T(8,128)(2,1)S(1)}, u32[]{:S(2)}, u32[]{:S(2)}) collective-permute-start(bf16[4,2,64,384]{3,2,1,0:T(8,128)(2,1)} %collective-permute-done.10.refs_9_), channel_id=1, source_target_pairs={{0,4},{1,5},{2,6},{3,7},{4,8},{5,9},{6,10},{7,11},{8,12},{9,13},{1... | collective-permute-start | bytes 1179656 | tf_op jit(solution)/shard_map/ppermute | solution.py:32
  64.9 41.6 %collective-permute-start = (bf16[128,4096]{1,0:T(8,128)(2,1)}, bf16[128,4096]{1,0:T(8,128)(2,1)S(1)}, u32[]{:S(2)}, u32[]{:S(2)}) collective-permute-start(bf16[128,4096]{1,0:T(8,128)(2,1)} %shard_map.120.refs_0_), channel_id=1, source_target_pairs={{0,1},{1,0},{2,3},{3,2},{4,5},{5,4},{6,7},{7,6},{8,9},{9,8},{10,11... | collective-permute-start | bytes 3145736 | tf_op jit(solution)/shard_map/ppermute | solution.py:32
  74.1 32.5 %collective-permute-start.1 = (bf16[128,4096]{1,0:T(8,128)(2,1)S(1)}, bf16[128,4096]{1,0:T(8,128)(2,1)S(1)}, u32[]{:S(2)}, u32[]{:S(2)}) collective-permute-start(bf16[128,4096]{1,0:T(8,128)(2,1)S(1)} %copy-done.1), channel_id=1, source_target_pairs={{0,1},{1,0},{2,3},{3,2},{4,5},{5,4},{6,7},{7,6},{8,9},{9,8},{10,11... | collective-permute-start | bytes 3145736 | tf_op jit(solution)/shard_map/ppermute | solution.py:32
  74.1 14.2 %collective-permute-start.25 = (bf16[5,2,64,384]{3,2,1,0:T(8,128)(2,1)}, bf16[5,2,64,384]{3,2,1,0:T(8,128)(2,1)S(1)}, u32[]{:S(2)}, u32[]{:S(2)}) collective-permute-start(bf16[5,2,64,384]{3,2,1,0:T(8,128)(2,1)} %bitcast_dynamic-update-slice_fusion.refs_17_), channel_id=1, source_target_pairs={{0,32},{1,33},{2,34},{3,35},{4,36},{5,37},{6,38},{7,39},{8,40},{9,... | collective-permute-start | bytes 1474568 | tf_op jit(solution)/shard_map/ppermute | solution.py:32
  88.3 22.6 %collective-permute-start.32 = (bf16[2,320,512]{2,1,0:T(8,128)(2,1)}, bf16[2,320,512]{2,1,0:T(8,128)(2,1)S(1)}, u32[]{:S(2)}, u32[]{:S(2)}) collective-permute-start(bf16[2,320,512]{2,1,0:T(8,128)(2,1)} %collective-permute-done.31.refs_26_), channel_id=1, source_target_pairs={{0,1},{1,0},{2,3},{3,2},{4,5},{5,4},{6,7},{7,6},{8,9},{9,8},{10,11... | collective-permute-start | bytes 1966088 | tf_op jit(solution)/shard_map/ppermute | solution.py:32
  89.1 41.9 %collective-permute-start.4 = (bf16[128,4096]{1,0:T(8,128)(2,1)S(1)}, bf16[128,4096]{1,0:T(8,128)(2,1)S(1)}, u32[]{:S(2)}, u32[]{:S(2)}) collective-permute-start(bf16[128,4096]{1,0:T(8,128)(2,1)S(1)} %collective-permute-done.2.refs_4_), channel_id=1, source_target_pairs={{0,1},{1,0},{2,3},{3,2},{4,5},{5,4},{6,7},{7,6},{8,9},{9,8},{10,11... | collective-permute-start | bytes 3145736 | tf_op jit(solution)/shard_map/ppermute | solution.py:32
  106.5 24.6 %collective-permute-start.5 = (bf16[128,4096]{1,0:T(8,128)(2,1)S(1)}, bf16[128,4096]{1,0:T(8,128)(2,1)S(1)}, u32[]{:S(2)}, u32[]{:S(2)}) collective-permute-start(bf16[128,4096]{1,0:T(8,128)(2,1)S(1)} %collective-permute-done.3.refs_5_), channel_id=1, source_target_pairs={{0,1},{1,0},{2,3},{3,2},{4,5},{5,4},{6,7},{7,6},{8,9},{9,8},{10,11... | collective-permute-start | bytes 3145736 | tf_op jit(solution)/shard_map/ppermute | solution.py:32
  106.5 12.7 %collective-permute-start.14 = (bf16[4,2,64,384]{3,2,1,0:T(8,128)(2,1)S(1)}, bf16[4,2,64,384]{3,2,1,0:T(8,128)(2,1)S(1)}, u32[]{:S(2)}, u32[]{:S(2)}) collective-permute-start(bf16[4,2,64,384]{3,2,1,0:T(8,128)(2,1)S(1)} %collective-permute-done.12.refs_11_), channel_id=1, source_target_pairs={{0,4},{1,5},{2,6},{3,7},{4,8},{5,9},{6,10},{7,11},{8,12},{9,13},{1... | collective-permute-start | bytes 1179656 | tf_op jit(solution)/shard_map/ppermute | solution.py:32
  108.5 13.9 %collective-permute-start.29 = (bf16[5,2,64,384]{3,2,1,0:T(8,128)(2,1)}, bf16[5,2,64,384]{3,2,1,0:T(8,128)(2,1)S(1)}, u32[]{:S(2)}, u32[]{:S(2)}) collective-permute-start(bf16[5,2,64,384]{3,2,1,0:T(8,128)(2,1)} %collective-permute-done.27.refs_21_), channel_id=1, source_target_pairs={{0,96},{1,97},{2,98},{3,99},{4,100},{5,101},{6,102},{7,103},{8,104... | collective-permute-start | bytes 1474568 | tf_op jit(solution)/shard_map/ppermute | solution.py:32
  110.9 11.5 %collective-permute-start.15 = (bf16[4,2,64,384]{3,2,1,0:T(8,128)(2,1)}, bf16[4,2,64,384]{3,2,1,0:T(8,128)(2,1)S(1)}, u32[]{:S(2)}, u32[]{:S(2)}) collective-permute-start(bf16[4,2,64,384]{3,2,1,0:T(8,128)(2,1)} %collective-permute-done.13.refs_12_), channel_id=1, source_target_pairs={{0,28},{1,29},{2,30},{3,31},{4,0},{5,1},{6,2},{7,3},{8,4},{9,5},{1... | collective-permute-start | bytes 1179656 | tf_op jit(solution)/shard_map/ppermute | solution.py:32
  119.2 11.8 %collective-permute-start.16 = (bf16[4,2,64,384]{3,2,1,0:T(8,128)(2,1)S(1)}, bf16[4,2,64,384]{3,2,1,0:T(8,128)(2,1)S(1)}, u32[]{:S(2)}, u32[]{:S(2)}) collective-permute-start(bf16[4,2,64,384]{3,2,1,0:T(8,128)(2,1)S(1)} %collective-permute-done.14.refs_13_), channel_id=1, source_target_pairs={{0,4},{1,5},{2,6},{3,7},{4,8},{5,9},{6,10},{7,11},{8,12},{9,13},{1... | collective-permute-start | bytes 1179656 | tf_op jit(solution)/shard_map/ppermute | solution.py:32
  159.0 27.2 %all-to-all-start = ((bf16[256,2,256]{2,1,0:T(2,128)(2,1)}), bf16[256,2,256]{2,1,0:T(2,128)(2,1)S(1)}, u32[]{:S(2)}, u32[]{:S(2)}) async-start(bf16[256,2,256]{2,1,0:T(2,128)(2,1)} %reshape.40), calls=%async_computation | async-start | bytes 524288 | tf_op jit(solution)/shard_map/all_to_all | solution.py:468
  171.4 22.0 %collective-permute-start.34 = (bf16[2,256,512]{2,1,0:T(8,128)(2,1)}, bf16[2,256,512]{2,1,0:T(8,128)(2,1)S(1)}, u32[]{:S(2)}, u32[]{:S(2)}) collective-permute-start(bf16[2,256,512]{2,1,0:T(8,128)(2,1)} %get-tuple-element.22), channel_id=1, source_target_pairs={{0,2},{1,3},{2,0},{3,1},{4,6},{5,7},{6,4},{7,5},{8,10},{9,11},{10,... | collective-permute-start | bytes 1572872 | tf_op jit(solution)/shard_map/ppermute | solution.py:32
  187.5 19.1 %all-to-all-start.1 = ((bf16[64,2,1024]{2,1,0:T(2,128)(2,1)}), bf16[64,2,1024]{2,1,0:T(2,128)(2,1)S(1)}, u32[]{:S(2)}, u32[]{:S(2)}) async-start(bf16[64,2,1024]{2,1,0:T(2,128)(2,1)} %broadcast_in_dim.2), calls=%async_computation.1 | async-start | bytes 524288 | tf_op jit(solution)/shard_map/all_to_all | solution.py:57
  193.4 14.7 %collective-permute-start.35 = (bf16[2,256,512]{2,1,0:T(8,128)(2,1)S(1)}, bf16[2,256,512]{2,1,0:T(8,128)(2,1)S(1)}, u32[]{:S(2)}, u32[]{:S(2)}) collective-permute-start(bf16[2,256,512]{2,1,0:T(8,128)(2,1)S(1)} %collective-permute-done.34.refs_2_), channel_id=1, source_target_pairs={{0,1},{1,0},{2,3},{3,2},{4,5},{5,4},{6,7},{7,6},{8,9},{9,8},{10,11... | collective-permute-start | bytes 1572872 | tf_op jit(solution)/shard_map/ppermute | solution.py:32
  193.5 14.6 %collective-permute-start.33 = (bf16[256,512]{1,0:T(8,128)(2,1)}, bf16[256,512]{1,0:T(8,128)(2,1)}, u32[]{:S(2)}, u32[]{:S(2)}) collective-permute-start(bf16[256,512]{1,0:T(8,128)(2,1)} %get-tuple-element.21), channel_id=1, source_target_pairs={{0,1},{1,0},{2,3},{3,2},{4,5},{5,4},{6,7},{7,6},{8,9},{9,8},{10,11... | collective-permute-start | bytes 786440 | tf_op jit(solution)/shard_map/ppermute | solution.py:32
  (30 other events, 488.4 us)
